TPU v7x, 32 devices: a whole 2x2x4 slice. The times are simulated.
32 devices in a mesh: az: 4 (over y, x), rng: 8 (over z, core).
Axes of the slice: x: 2, y: 2, z: 4, core: 2. Of those that a mesh axis runs over, the one named last changes fastest.
Arguments:
- echoes: bfloat16 [2, 256, 32, 1024], P(None, 'az', None, 'rng'), may hold values from -12 to 12
- arc_start: int32 [64], replicated, may hold values from 0 to 255, as said below
- arc_offsets: int32 [64, 16], replicated, may hold values from 0 to 63, as said below
- doppler_bins: int32 [64, 16], replicated, may hold values from 0 to 31
- steer_angles: float32 [64, 16], replicated, may hold values from -3.140625 to 3.140625
- train_mask: int32 [64, 8], P('az', 'rng'), may hold values from 0 to 1, as said below
Outputs:
- smoothed: float32 [64, 16, 1024], P('az', None, 'rng')
Inputs may be any that keep to these rules, and one draw needn't show every extreme that they name: `arc_start`: beam b's arc begins at column (b * 4 - 64 / 2 + j) mod 256 for some j with 0 <= j < 4. `arc_offsets`: each row holds 16 distinct offsets, ascending. `train_mask`: the last block of every beam is a training block.
All inputs are finite; a program needn't handle non-finite values.
Results may differ from a plain program's by a relative error of at most 0.0035.
Values may be sent and summed in bfloat16 or wider, within the bound.
A program may use at most 64 MiB of HBM per device.

v0:
```python
import functools

import jax
import jax.numpy as jnp
from jax import lax
from jax.experimental import pallas as pl
from jax.experimental.pallas import tpu as pltpu
from jax.sharding import PartitionSpec as P


COLS = 256
ARC = 64
BINS = 3
BEAMS = 64
BLK = 128
LOADING = 0.1
VMEM_LIMIT = 48 << 20
CHAIN_VMEM = 66_200_000


def doppler_table(num_pulses):
    freq_ids = jnp.arange(num_pulses, dtype=jnp.int32)
    phase_steps = freq_ids[:, None] * freq_ids[None, :] % num_pulses
    phase_angle = -2.0 * jnp.pi / num_pulses * phase_steps.astype(jnp.float32)
    return (jnp.cos(phase_angle).astype(jnp.bfloat16), jnp.sin(phase_angle).astype(jnp.bfloat16))


def snap_gram_kernel(
    col_ref, bins_ref, cos_ref, sin_ref, ext_ref, table_ref, mask_ref, v_ref, gram_ref
):
    beam = pl.program_id(0)
    pulses = ext_ref.shape[2]
    num_sel = col_ref.shape[1]
    num_chan = bins_ref.shape[1]
    table = table_ref[...]
    parts_re, parts_im = [], []
    for j in range(num_sel):
        col = col_ref[beam, j]
        data = jnp.concatenate([ext_ref[0, col], ext_ref[1, col]], axis=0)
        spec = jnp.dot(table, data, preferred_element_type=jnp.float32)
        cosine = cos_ref[beam, j]
        sine = sin_ref[beam, j]
        spec_re = spec[:pulses]
        spec_im = spec[pulses:]
        parts_re.append(cosine * spec_re - sine * spec_im)
        parts_im.append(sine * spec_re + cosine * spec_im)
    for part, pieces in enumerate((parts_re, parts_im)):
        stacked = jnp.swapaxes(jnp.stack(pieces, 0), 0, 1)
        v_ref[0, part] = stacked.astype(jnp.bfloat16)
    dof = BINS * num_sel
    mask_row = mask_ref[0]
    row = lax.broadcasted_iota(jnp.int32, (dof, dof), 0)
    colm = lax.broadcasted_iota(jnp.int32, (dof, dof), 1)
    lower = row >= colm
    packed = []
    for k in range(num_chan):
        centre = bins_ref[beam, k]
        ids = [(centre + (q - BINS // 2 + pulses)) % pulses for q in range(BINS)]
        u_re = jnp.concatenate([v_ref[0, 0, f] for f in ids], 0)
        u_im = jnp.concatenate([v_ref[0, 1, f] for f in ids], 0)
        right = jnp.concatenate([u_re, u_im], 1)
        m_re = u_re * mask_row
        m_im = u_im * mask_row
        left = jnp.concatenate(
            [jnp.concatenate([m_re, m_im], 1), jnp.concatenate([m_im, -m_re], 1)], 0
        )
        both = lax.dot_general(
            left, right, (((1,), (1,)), ((), ())), preferred_element_type=jnp.float32
        )
        packed.append(jnp.where(lower, both[:dof], both[dof:]))
    gram_ref[0] = jnp.concatenate(packed, 1)


def solve_kernel(part_ref, out_ref, stack, turned, hr, hi, xr, xi):
    lead, dof, wide = part_ref.shape
    width = wide // dof
    lanes = lead * width
    nb = dof // 8
    group = min(8, lanes)
    for g in range(0, lanes, group):
        pieces = []
        for item in range(g, g + group):
            k = item % width
            pieces.append(part_ref[item // width, :, k * dof : (k + 1) * dof])
        stack[:, g : g + group, :] = jnp.swapaxes(jnp.stack(pieces, 0), 0, 1)
    for i in range(dof):
        turned[i] = stack[i].T
    trace = jnp.zeros((1, lanes), jnp.float32)
    for i in range(dof):
        trace = trace + turned[i, i : i + 1, :]
    load = (LOADING / dof) * trace
    cube = (8, 8, lanes)
    row = lax.broadcasted_iota(jnp.int32, cube, 0)
    col = lax.broadcasted_iota(jnp.int32, cube, 1)
    for ib in range(nb):
        rows = slice(8 * ib, 8 * ib + 8)
        for jb in range(ib, nb):
            cols = slice(8 * jb, 8 * jb + 8)
            imag = turned[rows, cols, :]
            real = jnp.swapaxes(turned[cols, rows, :], 0, 1)
            if ib == jb:
                straight, flip = imag, real
                real = jnp.where(row >= col, straight, flip)
                real = jnp.where(row == col, real + load[None], real)
                imag = jnp.where(row < col, straight, jnp.where(row > col, -flip, 0.0))
            hr[rows, cols, :] = real
            hi[rows, cols, :] = imag
    hr[:, dof:, :] = jnp.ones((dof, 8, lanes), jnp.float32)
    hi[:, dof:, :] = jnp.zeros((dof, 8, lanes), jnp.float32)
    xr[...] = jnp.zeros_like(xr)
    xi[...] = jnp.zeros_like(xi)
    sub = lax.broadcasted_iota(jnp.int32, (8, lanes), 0)

    for kb in range(nb):

        def step(k, carry, kb=kb):
            pivot = 1.0 / hr[k, pl.ds(k, 1), :]
            rr = [hr[k, 8 * b : 8 * b + 8, :] for b in range(kb, nb + 1)]
            ri = [hi[k, 8 * b : 8 * b + 8, :] for b in range(kb, nb + 1)]
            for ib in range(kb, nb):
                fr = rr[ib - kb] * pivot
                fi = -ri[ib - kb] * pivot
                if ib == kb:
                    live = sub + 8 * kb > k
                    fr = jnp.where(live, fr, 0.0)
                    fi = jnp.where(live, fi, 0.0)
                for s in range(8):
                    i = 8 * ib + s
                    cr = jnp.broadcast_to(fr[s : s + 1], (8, lanes))
                    ci = jnp.broadcast_to(fi[s : s + 1], (8, lanes))
                    for b in range(ib, nb + 1):
                        pr, pi = rr[b - kb], ri[b - kb]
                        sl = slice(8 * b, 8 * b + 8)
                        hr[i, sl, :] = hr[i, sl, :] - (cr * pr - ci * pi)
                        hi[i, sl, :] = hi[i, sl, :] - (cr * pi + ci * pr)
            return carry

        lax.fori_loop(8 * kb, 8 * kb + 8, step, 0)

    for ib in reversed(range(nb)):

        def back(t, carry, ib=ib):
            i = 8 * ib + 7 - t
            sr = jnp.zeros((8, lanes), jnp.float32)
            si = jnp.zeros((8, lanes), jnp.float32)
            for b in range(ib, nb):
                sl = slice(8 * b, 8 * b + 8)
                ar, ai = hr[i, sl, :], hi[i, sl, :]
                br, bi = xr[sl, :], xi[sl, :]
                sr = sr + (ar * br - ai * bi)
                si = si + (ar * bi + ai * br)
            pivot = 1.0 / hr[i, pl.ds(i, 1), :]
            top_r = hr[i, dof : dof + 1, :]
            top_i = hi[i, dof : dof + 1, :]
            xr[pl.ds(i, 1), :] = (top_r - jnp.sum(sr, 0, keepdims=True)) * pivot
            xi[pl.ds(i, 1), :] = (top_i - jnp.sum(si, 0, keepdims=True)) * pivot
            return carry

        lax.fori_loop(0, 8, back, 0)
    out_ref[:dof, :lanes] = xr[...]
    out_ref[dof : 2 * dof, :lanes] = xi[...]
    out_ref[2 * dof : 2 * dof + 8, :lanes] = jnp.broadcast_to(
        jnp.sum(xr[...], 0, keepdims=True), (8, lanes)
    )


MESH = pl.DeviceIdType.MESH


def scatter_kernel(n, halves, *refs):
    g_refs = refs[:halves]
    out_ref, pair, acc, right, left, psend, precv, rsend, rrecv, lsend, lrecv = refs[halves:]
    share = n // halves

    def own(t, core):
        return g_refs[t // share].at[2 * (t % share) + core]

    me = lax.axis_index("rng")
    z = me // 2
    c = me % 2
    mate = 2 * z + 1 - c
    ahead = lax.rem(me + 2, 2 * n)
    behind = lax.rem(me + 2 * n - 2, 2 * n)
    barrier = pltpu.get_barrier_semaphore()
    pl.semaphore_signal(barrier, inc=1, device_id={"rng": mate}, device_id_type=MESH)
    pl.semaphore_signal(barrier, inc=1, device_id={"rng": ahead}, device_id_type=MESH)
    pl.semaphore_signal(barrier, inc=1, device_id={"rng": behind}, device_id_type=MESH)
    pl.semaphore_wait(barrier, 3)

    order = []
    for t in range((n + 1) // 2):
        order.append(n - 1 - t)
        if t != n - 1 - t:
            order.append(t)

    def pair_copy(t):
        return pltpu.make_async_remote_copy(
            src_ref=own(t, 1 - c),
            dst_ref=pair.at[t],
            send_sem=psend.at[t],
            recv_sem=precv.at[t],
            device_id={"rng": mate},
            device_id_type=MESH,
        )

    def right_copy(t):
        return pltpu.make_async_remote_copy(
            src_ref=acc.at[t],
            dst_ref=right.at[t],
            send_sem=rsend.at[t],
            recv_sem=rrecv.at[t],
            device_id={"rng": ahead},
            device_id_type=MESH,
        )

    def left_copy(t):
        return pltpu.make_async_remote_copy(
            src_ref=acc.at[t],
            dst_ref=left.at[t],
            send_sem=lsend.at[t],
            recv_sem=lrecv.at[t],
            device_id={"rng": behind},
            device_id_type=MESH,
        )

    for t in order:
        pair_copy(t).start()
    for t in order:
        pair_copy(t).wait_recv()
        acc[t] = own(t, c)[...] + pair[t]

        @pl.when(jnp.logical_and(z == 0, t > 0))
        def _(t=t):
            right_copy(t).start()

        @pl.when(jnp.logical_and(z == n - 1, t < n - 1))
        def _(t=t):
            left_copy(t).start()

    for place in range(n):
        events = [(place + n - 1 - t, 0, t) for t in range(place + 1, n) if place > 0]
        events += [(n - 1 - place + t, 1, t) for t in range(place) if place < n - 1]

        @pl.when(z == place)
        def _(place=place, events=sorted(events)):
            for _, side, t in events:
                copy = left_copy(t) if side else right_copy(t)
                source = left if side else right
                copy.wait_recv()
                acc[t] = acc[t] + source[t]
                copy.start()
            total = acc[place]
            if place > 0:
                right_copy(place).wait_recv()
                total = total + right[place]
            if place < n - 1:
                left_copy(place).wait_recv()
                total = total + left[place]
            out_ref[...] = total

    for t in range(n):
        pair_copy(t).wait_send()

        @pl.when(z < t)
        def _(t=t):
            right_copy(t).wait_send()

        @pl.when(z > t)
        def _(t=t):
            left_copy(t).wait_send()


def apply_kernel(
    halves,
    per,
    dof,
    pay_ref,
    bins_ref,
    *refs,
):
    v_refs = refs[:halves]
    (out_ref, v_all, gat, power, edge, halo, sums, az_lo, az_hi) = refs[halves : halves + 9]
    (vsem, gsend, grecv, esend, erecv, asend, arecv) = refs[halves + 9 :]
    me = lax.axis_index("rng")
    az = lax.axis_index("az")
    n = lax.axis_size("rng")
    m = lax.axis_size("az")
    beams, num_chan, cells = out_ref.shape
    pulses, num_sel = v_all.shape[2], v_all.shape[3]
    taps = pulses * num_sel
    az_next = lax.rem(az + 1, m)
    az_prev = lax.rem(az + m - 1, m)
    barrier = pltpu.get_barrier_semaphore()
    for d in range(1, n):
        peer = lax.rem(me + d, n)
        pl.semaphore_signal(barrier, inc=1, device_id={"rng": peer}, device_id_type=MESH)
    for other in (az_next, az_prev):
        pl.semaphore_signal(barrier, inc=1, device_id={"az": other}, device_id_type=MESH)
    share = beams // halves
    loads = []
    for h in range(halves):
        load = pltpu.make_async_copy(v_refs[h], v_all.at[pl.ds(h * share, share)], vsem.at[h])
        load.start()
        loads.append(load)
    pl.semaphore_wait(barrier, n + 1)

    copies = []
    for d in range(1, n):
        peer = lax.rem(me + d, n)
        copy = pltpu.make_async_remote_copy(
            src_ref=pay_ref,
            dst_ref=gat.at[me],
            send_sem=gsend.at[d],
            recv_sem=grecv.at[d],
            device_id={"rng": peer},
            device_id_type=MESH,
        )
        copy.start()
        copies.append(copy)
    gat[me] = pay_ref[...]
    for load in loads:
        load.wait()
    for copy in copies:
        copy.wait_recv()
    rows = gat.shape[1] - beams
    count = jnp.zeros((beams, gat.shape[2]), jnp.float32)
    for r in range(n):
        count = count + gat[r, rows:, :]
    sums[0] = jnp.zeros(sums.shape[1:], jnp.float32)
    for b in range(beams):
        sums[b, :1, :] = count[b : b + 1]
    freq = lax.broadcasted_iota(jnp.int32, (num_chan, taps), 1) // num_sel
    lanes = gat.shape[2]
    lane = lax.broadcasted_iota(jnp.int32, (num_chan, lanes), 1)

    def one(b, carry):
        if per >= num_chan:
            ratio = per // num_chan
            start = pl.multiple_of((b % ratio) * num_chan, 8)
            w = gat[b // ratio, pl.ds(start, num_chan), :]
        else:
            split = num_chan // per
            w = jnp.concatenate([gat[b * split + t, :per, :] for t in range(split)], 0)
        w = w * sums[b, :1, :]
        quiet = w[:, 2 * dof : 2 * dof + 1]
        centre = bins_ref[b]
        planes = []
        hits = []
        for q in range(BINS):
            f = lax.rem(centre + (q - BINS // 2 + pulses), pulses)
            hits.append(freq == f)
        for part in range(2):
            plane = jnp.zeros((num_chan, taps), jnp.float32)
            for q in range(BINS):
                start = part * dof + q * num_sel
                piece = pltpu.roll(w, (lanes - start) % lanes, 1) if start else w
                piece = jnp.where(lane < num_sel, piece, 0.0)
                span = num_sel
                while span < lanes:
                    piece = piece + pltpu.roll(piece, span, 1)
                    span *= 2
                tiled = jnp.concatenate([piece] * (taps // lanes), 1)
                plane = jnp.where(hits[q], tiled, plane)
            planes.append(plane)
        top = jnp.concatenate([planes[0], planes[1]], 1)
        low = jnp.concatenate([-planes[1], planes[0]], 1)
        lhs = jnp.concatenate([top, low], 0).astype(jnp.bfloat16)
        flat = v_all[b].reshape(2 * taps, cells)
        proj = jnp.dot(lhs, flat, preferred_element_type=jnp.float32)
        p0 = proj[:num_chan]
        p1 = proj[num_chan:]
        power[b] = (p0 * p0 + p1 * p1) / quiet
        return carry

    lax.fori_loop(0, beams, one, 0)
    items = beams * num_chan
    turned = power[...].reshape(items, cells).T
    edge[0] = turned[:8]
    edge[1] = turned[cells - 8 :]

    def edge_copy(side):
        target = lax.rem(me + 1, n) if side else lax.rem(me + n - 1, n)
        return pltpu.make_async_remote_copy(
            src_ref=edge.at[side],
            dst_ref=halo.at[side],
            send_sem=esend.at[side],
            recv_sem=erecv.at[side],
            device_id={"rng": target},
            device_id_type=MESH,
        )

    for side in range(2):
        edge_copy(side).start()
    for side in range(2):
        edge_copy(side).wait()
    before = jnp.where(me > 0, halo[1, 7:8], 0.0)
    after = jnp.where(me < n - 1, halo[0, 0:1], 0.0)
    turned = (
        jnp.concatenate([before, turned[:-1]], 0)
        + turned
        + jnp.concatenate([turned[1:], after], 0)
    )
    sums[...] = turned.T.reshape(beams, num_chan, cells)
    up = pltpu.make_async_remote_copy(
        src_ref=sums.at[beams - 1],
        dst_ref=az_lo,
        send_sem=asend.at[0],
        recv_sem=arecv.at[0],
        device_id={"az": az_next},
        device_id_type=MESH,
    )
    down = pltpu.make_async_remote_copy(
        src_ref=sums.at[0],
        dst_ref=az_hi,
        send_sem=asend.at[1],
        recv_sem=arecv.at[1],
        device_id={"az": az_prev},
        device_id_type=MESH,
    )
    up.start()
    down.start()
    for b in range(1, beams - 1):
        out_ref[b] = (sums[b - 1] + sums[b] + sums[b + 1]) / 9.0
    up.wait_recv()
    down.wait_recv()
    out_ref[0] = (az_lo[...] + sums[0] + sums[1]) / 9.0
    out_ref[beams - 1] = (sums[beams - 2] + sums[beams - 1] + az_hi[...]) / 9.0
    up.wait_send()
    down.wait_send()
    for copy in copies:
        copy.wait_send()


def gram_of(v_ref, beam, bins, mask_row):
    pulses = v_ref.shape[2]
    num_sel = v_ref.shape[3]
    dof = BINS * num_sel
    row = lax.broadcasted_iota(jnp.int32, (dof, dof), 0)
    colm = lax.broadcasted_iota(jnp.int32, (dof, dof), 1)
    lower = row >= colm
    packed = []
    for centre in bins:
        ids = [lax.rem(centre + (q - BINS // 2 + pulses), pulses) for q in range(BINS)]
        u_re = jnp.concatenate([v_ref[beam, 0, f] for f in ids], 0)
        u_im = jnp.concatenate([v_ref[beam, 1, f] for f in ids], 0)
        right = jnp.concatenate([u_re, u_im], 1)
        m_re = u_re * mask_row
        m_im = u_im * mask_row
        left = jnp.concatenate(
            [jnp.concatenate([m_re, m_im], 1), jnp.concatenate([m_im, -m_re], 1)], 0
        )
        both = lax.dot_general(
            left, right, (((1,), (1,)), ((), ())), preferred_element_type=jnp.float32
        )
        packed.append(jnp.where(lower, both[:dof], both[dof:]))
    return packed


def chain_kernel(
    early,
    start_ref,
    offs_ref,
    bins_ref,
    cos_ref,
    sin_ref,
    echoes,
    table_ref,
    mask_ref,
    chan_ref,
    out_ref,
    ext,
    low,
    high,
    v_all,
    gram,
    pair,
    acc,
    ring,
    direct,
    part,
    solved,
    stack,
    turned,
    hr,
    hi,
    xr,
    xi,
    masks,
    counts,
    pay,
    gat_e,
    gat_l,
    wts_e,
    wts_l,
    pw,
    pl_left,
    pl_right,
    rows,
    esem,
    hsend,
    hrecv,
    psend,
    precv,
    rsend,
    rrecv,
    dsend,
    drecv,
    msend,
    mrecv,
    gsend,
    grecv_e,
    grecv_l,
    lsend,
    lrecv,
    tsend,
    trecv,
    asend,
    arecv,
):
    me = lax.axis_index("rng")
    az = lax.axis_index("az")
    size = lax.axis_size("rng")
    m = lax.axis_size("az")
    n = size // 2
    z = me // 2
    c = lax.rem(me, 2)
    beams, num_chan, cells = out_ref.shape
    columns = echoes.shape[1]
    pulses = echoes.shape[2]
    num_sel = offs_ref.shape[0]
    dof = BINS * num_sel
    taps = pulses * num_sel
    steps = beams // 2
    late = steps - early
    width = ARC // 2
    w = width // steps
    side_chan = num_chan // 2
    az_next = lax.rem(az + 1, m)
    az_prev = lax.rem(az + m - 1, m)
    ahead = lax.rem(me + 1, size)
    behind = lax.rem(me + size - 1, size)
    mid_l = n // 2 - 1
    mid_r = n // 2
    is_end = jnp.logical_or(z == 0, z == n - 1)
    is_mid = jnp.logical_or(z == mid_l, z == mid_r)

    own_cols = pltpu.make_async_copy(echoes, ext.at[:, width : width + columns], esem)
    own_cols.start()
    pl_left[...] = jnp.zeros(pl_left.shape, jnp.float32)
    pl_right[...] = jnp.zeros(pl_right.shape, jnp.float32)
    barrier = pltpu.get_barrier_semaphore()
    for d in range(1, size):
        peer = lax.rem(me + d, size)
        pl.semaphore_signal(barrier, inc=1, device_id={"rng": peer}, device_id_type=MESH)
    for other in (az_next, az_prev):
        pl.semaphore_signal(barrier, inc=1, device_id={"az": other}, device_id_type=MESH)
        for r in (ahead, behind):
            pl.semaphore_signal(
                barrier, inc=1, device_id={"az": other, "rng": r}, device_id_type=MESH
            )
    pl.semaphore_wait(barrier, size + 5)

    def low_copy(i):
        return pltpu.make_async_remote_copy(
            src_ref=echoes.at[:, pl.ds(columns - w * (i + 1), w)],
            dst_ref=low.at[i],
            send_sem=hsend.at[0, i],
            recv_sem=hrecv.at[0, i],
            device_id={"az": az_next},
            device_id_type=MESH,
        )

    def high_copy(i):
        return pltpu.make_async_remote_copy(
            src_ref=echoes.at[:, pl.ds(w * i, w)],
            dst_ref=high.at[i],
            send_sem=hsend.at[1, i],
            recv_sem=hrecv.at[1, i],
            device_id={"az": az_prev},
            device_id_type=MESH,
        )

    for i in range(steps):
        low_copy(i).start()
        high_copy(i).start()

    def mask_copy(d):
        return pltpu.make_async_remote_copy(
            src_ref=mask_ref,
            dst_ref=masks.at[me],
            send_sem=msend.at[d],
            recv_sem=mrecv.at[me],
            device_id={"rng": lax.rem(me + d, size)},
            device_id_type=MESH,
        )

    for d in range(1, size):
        mask_copy(d).start()
    masks[me] = mask_ref[...]

    part[...] = jnp.zeros(part.shape, jnp.float32)
    solved[...] = jnp.zeros(solved.shape, jnp.float32)
    own_cols.wait()

    def mine(t):
        return jnp.where(c == 0, steps - 1 - t, steps + t)

    def pair_copy(t):
        return pltpu.make_async_remote_copy(
            src_ref=gram.at[jnp.where(c == 0, steps + t, steps - 1 - t)],
            dst_ref=pair.at[t],
            send_sem=psend.at[t],
            recv_sem=precv.at[t],
            device_id={"rng": 2 * z + 1 - c},
            device_id_type=MESH,
        )

    def ring_copy(side, t):
        target = lax.rem(me + 2, size) if side else lax.rem(me + size - 2, size)
        return pltpu.make_async_remote_copy(
            src_ref=acc.at[t, side],
            dst_ref=ring.at[side, t],
            send_sem=rsend.at[side, t],
            recv_sem=rrecv.at[side, t],
            device_id={"rng": target},
            device_id_type=MESH,
        )

    def direct_copy(side, t, source):
        owner = 2 * (mid_r if side else mid_l) + c
        return pltpu.make_async_remote_copy(
            src_ref=acc.at[t, side],
            dst_ref=direct.at[t - early, source],
            send_sem=dsend.at[t - early, side],
            recv_sem=drecv.at[t - early, source],
            device_id={"rng": owner},
            device_id_type=MESH,
        )

    table = table_ref[...]

    def one_beam(b):
        bg = az * beams + b
        first = lax.rem(start_ref[bg] - az * columns + (width + COLS), COLS)
        first = jnp.minimum(first, ext.shape[1] - ARC)
        parts_re, parts_im = [], []
        for j in range(num_sel):
            col = first + offs_ref[j, bg]
            data = jnp.concatenate([ext[0, col], ext[1, col]], axis=0)
            spec = jnp.dot(table, data, preferred_element_type=jnp.float32)
            cosine = cos_ref[j, bg]
            sine = sin_ref[j, bg]
            spec_re = spec[:pulses]
            spec_im = spec[pulses:]
            parts_re.append(cosine * spec_re - sine * spec_im)
            parts_im.append(sine * spec_re + cosine * spec_im)
        for p, pieces in enumerate((parts_re, parts_im)):
            stacked = jnp.swapaxes(jnp.stack(pieces, 0), 0, 1)
            v_all[b, p] = stacked.astype(jnp.bfloat16)
        mask_row = mask_ref[pl.ds(b, 1), :].astype(jnp.bfloat16)
        bins = [bins_ref[k, bg] for k in range(num_chan)]
        packed = gram_of(v_all, b, bins, mask_row)
        gram[b, 0] = jnp.concatenate(packed[:side_chan], 1)
        gram[b, 1] = jnp.concatenate(packed[side_chan:], 1)

    def slot(s, carry):
        @pl.when(s < steps)
        def _():
            low_copy(s).wait_recv()
            high_copy(s).wait_recv()
            ext[:, pl.ds(width - w * (s + 1), w)] = low[s]
            ext[:, pl.ds(width + columns + w * s, w)] = high[s]

            def two(i, carry):
                one_beam(jnp.where(i == 0, steps - 1 - s, steps + s))
                return carry

            lax.fori_loop(0, 2, two, 0)
            pair_copy(s).start()

        t = s - 1

        @pl.when(jnp.logical_and(t >= 0, t < steps))
        def _():
            pair_copy(t).wait_recv()
            own = mine(t)
            acc[t] = gram[own] + pair[t]

            @pl.when(t < early)
            def _():
                @pl.when(z == 0)
                def _():
                    ring_copy(1, t).start()

                @pl.when(z == n - 1)
                def _():
                    ring_copy(0, t).start()

            @pl.when(t >= early)
            def _():
                for side, owner in ((0, mid_l), (1, mid_r)):

                    @pl.when(z != owner)
                    def _(side=side):
                        direct_copy(side, t, z).start()

        for side in range(2):
            place = z if side else n - 1 - z
            tt = s - 1 - place

            @pl.when(jnp.logical_and(place > 0, jnp.logical_and(tt >= 0, tt < early)))
            def _(side=side, place=place, tt=tt):
                ring_copy(side, tt).wait_recv()
                total = acc[tt, side] + ring[side, tt]

                @pl.when(place < n - 1)
                def _():
                    acc[tt, side] = total
                    ring_copy(side, tt).start()

                @pl.when(place == n - 1)
                def _():
                    part[tt] = total

        return carry

    lax.fori_loop(0, max(steps + 1, early + n), slot, 0)

    for side, owner in ((0, mid_l), (1, mid_r)):

        @pl.when(z == owner)
        def _(side=side, owner=owner):
            for i in range(late):
                total = acc[early + i, side]
                for source in range(n):
                    if source != owner:
                        direct_copy(side, early + i, source).wait_recv()
                        total = total + direct[i, source]
                part[i] = total

    for d in range(1, size):
        src = lax.rem(me + d, size)
        pltpu.make_async_remote_copy(
            src_ref=mask_ref,
            dst_ref=masks.at[src],
            send_sem=msend.at[d],
            recv_sem=mrecv.at[src],
            device_id={"rng": src},
            device_id_type=MESH,
        ).wait_recv()
    all_masks = masks[0]
    for r in range(1, size):
        all_masks = all_masks + masks[r]
    counts[...] = jnp.broadcast_to(jnp.sum(all_masks, 1, keepdims=True), counts.shape)

    solve_kernel(part, solved, stack, turned, hr, hi, xr, xi)
    lanes = pay.shape[1]
    flipped = solved[...].T
    items = early * side_chan
    scaled = []
    for t in range(early):
        tt = jnp.where(is_mid, early + jnp.minimum(t, late - 1), t)
        scaled.append(
            flipped[side_chan * t : side_chan * (t + 1)] * counts[pl.ds(mine(tt), 1), :]
        )
    full = jnp.concatenate(scaled, 0)
    lane = lax.broadcasted_iota(jnp.int32, (items, lanes), 1)
    hi_part = full.astype(jnp.bfloat16).astype(jnp.float32)
    rest = full - hi_part
    mid_part = rest.astype(jnp.bfloat16).astype(jnp.float32)
    lo_part = rest - mid_part
    coded = jnp.where(
        lane == 2 * dof + 1, mid_part, jnp.where(lane == 2 * dof + 2, lo_part, hi_part)
    )
    pay[...] = coded.astype(jnp.bfloat16)

    def end_copy(d, side):
        return pltpu.make_async_remote_copy(
            src_ref=pay,
            dst_ref=gat_e.at[side, c],
            send_sem=gsend.at[d],
            recv_sem=grecv_e.at[side, c],
            device_id={"rng": lax.rem(me + d, size)},
            device_id_type=MESH,
        )

    def mid_copy(d, side):
        return pltpu.make_async_remote_copy(
            src_ref=pay.at[: late * side_chan],
            dst_ref=gat_l.at[side, c],
            send_sem=gsend.at[d],
            recv_sem=grecv_l.at[side, c],
            device_id={"rng": lax.rem(me + d, size)},
            device_id_type=MESH,
        )

    for side, owner in ((0, 0), (1, n - 1)):

        @pl.when(z == owner)
        def _(side=side):
            for d in range(1, size):
                end_copy(d, side).start()
            gat_e[side, c] = pay[...]

    for side, owner in ((0, mid_l), (1, mid_r)):

        @pl.when(z == owner)
        def _(side=side):
            for d in range(1, size):
                mid_copy(d, side).start()
            gat_l[side, c] = pay[: late * side_chan]

    freq = (lax.broadcasted_iota(jnp.int32, (num_chan, taps), 1) // num_sel).astype(jnp.float32)
    blane = lax.broadcasted_iota(jnp.int32, chan_ref.shape, 1)
    wlane = lax.broadcasted_iota(jnp.int32, (num_chan, lanes), 1)

    def tile_copy(side, b):
        target = ahead if side else behind
        buf = pl_left if side else pl_right
        return pltpu.make_async_remote_copy(
            src_ref=pw.at[b + 1],
            dst_ref=buf.at[b + 1],
            send_sem=lsend.at[side, b],
            recv_sem=lrecv.at[side, b],
            device_id={"rng": target},
            device_id_type=MESH,
        )

    def az_copy(up):
        return pltpu.make_async_remote_copy(
            src_ref=pw.at[beams if up else 1],
            dst_ref=pw.at[0 if up else beams + 1],
            send_sem=tsend.at[up],
            recv_sem=trecv.at[up],
            device_id={"az": az_next if up else az_prev},
            device_id_type=MESH,
        )

    def corner_copy(up, side):
        buf = pl_left if side else pl_right
        return pltpu.make_async_remote_copy(
            src_ref=pw.at[beams if up else 1],
            dst_ref=buf.at[0 if up else beams + 1],
            send_sem=asend.at[up, side],
            recv_sem=arecv.at[up, side],
            device_id={
                "az": az_next if up else az_prev,
                "rng": ahead if side else behind,
            },
            device_id_type=MESH,
        )

    def one_power(b, wt):
        quiet = wt[:, 2 * dof : 2 * dof + 1]
        quiet = quiet + wt[:, 2 * dof + 1 : 2 * dof + 2] + wt[:, 2 * dof + 2 : 2 * dof + 3]
        centre = jnp.sum(
            jnp.where(blane == az * beams + b, chan_ref[...], 0.0), 1, keepdims=True
        )
        hits = []
        for q in range(BINS):
            f = centre + (q - BINS // 2)
            f = jnp.where(f < 0.0, f + pulses, jnp.where(f >= pulses, f - pulses, f))
            hits.append(freq == f)
        planes = []
        for p in range(2):
            plane = jnp.zeros((num_chan, taps), jnp.float32)
            for q in range(BINS):
                start = p * dof + q * num_sel
                piece = pltpu.roll(wt, (lanes - start) % lanes, 1) if start else wt
                piece = jnp.where(wlane < num_sel, piece, 0.0)
                span = num_sel
                while span < lanes:
                    piece = piece + pltpu.roll(piece, span, 1)
                    span *= 2
                tiled = jnp.concatenate([piece] * (taps // lanes), 1)
                plane = jnp.where(hits[q], tiled, plane)
            planes.append(plane)
        top = jnp.concatenate([planes[0], planes[1]], 1)
        bottom = jnp.concatenate([-planes[1], planes[0]], 1)
        lhs = jnp.concatenate([top, bottom], 0).astype(jnp.bfloat16)
        flat = v_all[b].reshape(2 * taps, cells)
        proj = jnp.dot(lhs, flat, preferred_element_type=jnp.float32)
        p0 = proj[:num_chan]
        p1 = proj[num_chan:]
        pw[b + 1] = (p0 * p0 + p1 * p1) / quiet

        @pl.when(me < size - 1)
        def _():
            tile_copy(1, b).start()

        @pl.when(me > 0)
        def _():
            tile_copy(0, b).start()

    def gathered(sem, buf, side, owner, copy):
        for core in range(2):

            @pl.when(me != 2 * owner + core)
            def _(core=core):
                pltpu.make_async_remote_copy(
                    src_ref=copy,
                    dst_ref=buf.at[side, core],
                    send_sem=gsend.at[0],
                    recv_sem=sem.at[side, core],
                    device_id={"rng": ahead},
                    device_id_type=MESH,
                ).wait_recv()

    gathered(grecv_e, gat_e, 0, 0, pay)
    gathered(grecv_e, gat_e, 1, n - 1, pay)
    wts_e[...] = gat_e[...].astype(jnp.float32)

    def weights(buf, i, core):
        start = pl.multiple_of(i * side_chan, side_chan)
        return jnp.concatenate(
            [buf[0, core, pl.ds(start, side_chan), :], buf[1, core, pl.ds(start, side_chan), :]], 0
        )

    def early_power(i, carry):
        t = i // 2
        core = lax.rem(i, 2)
        one_power(jnp.where(core == 0, steps - 1 - t, steps + t), weights(wts_e, t, core))
        return carry

    lax.fori_loop(0, 2 * early, early_power, 0)
    short = pay.at[: late * side_chan]
    gathered(grecv_l, gat_l, 0, mid_l, short)
    gathered(grecv_l, gat_l, 1, mid_r, short)
    wts_l[...] = gat_l[...].astype(jnp.float32)

    def late_power(i, carry):
        t = late - 1 - i // 2
        core = lax.rem(i, 2)
        one_power(
            jnp.where(core == 0, late - 1 - t, steps + early + t), weights(wts_l, t, core)
        )

        @pl.when(i == 0)
        def _():
            az_copy(0).start()

            @pl.when(me < size - 1)
            def _():
                corner_copy(0, 1).start()

            @pl.when(me > 0)
            def _():
                corner_copy(0, 0).start()

        @pl.when(i == 1)
        def _():
            az_copy(1).start()

            @pl.when(me < size - 1)
            def _():
                corner_copy(1, 1).start()

            @pl.when(me > 0)
            def _():
                corner_copy(1, 0).start()

        return carry

    lax.fori_loop(0, 2 * late, late_power, 0)

    lane = lax.broadcasted_iota(jnp.int32, (num_chan, cells), 1)

    def row_sum(i):
        mid = pw[i]
        back = pltpu.roll(jnp.where(lane == cells - 1, pl_left[i], mid), 1, 1)
        fore = pltpu.roll(jnp.where(lane == 0, pl_right[i], mid), cells - 1, 1)
        return back + mid + fore

    for b in range(beams):

        @pl.when(me > 0)
        def _(b=b):
            tile_copy(1, b).wait_recv()

        @pl.when(me < size - 1)
        def _(b=b):
            tile_copy(0, b).wait_recv()

    for b in range(beams):
        rows[b + 1] = row_sum(b + 1)
    for b in range(1, beams - 1):
        out_ref[b] = (rows[b] + rows[b + 1] + rows[b + 2]) / 9.0
    for up in range(2):
        az_copy(up).wait_recv()

        @pl.when(me > 0)
        def _(up=up):
            corner_copy(up, 1).wait_recv()

        @pl.when(me < size - 1)
        def _(up=up):
            corner_copy(up, 0).wait_recv()

    out_ref[0] = (row_sum(0) + rows[1] + rows[2]) / 9.0
    out_ref[beams - 1] = (rows[beams - 1] + rows[beams] + row_sum(beams + 1)) / 9.0

    for i in range(steps):
        low_copy(i).wait_send()
        high_copy(i).wait_send()
        pair_copy(i).wait_send()
    for i in range(early):

        @pl.when(z < n - 1)
        def _(i=i):
            ring_copy(1, i).wait_send()

        @pl.when(z > 0)
        def _(i=i):
            ring_copy(0, i).wait_send()

    for i in range(late):
        for side, owner in ((0, mid_l), (1, mid_r)):

            @pl.when(z != owner)
            def _(side=side, i=i):
                direct_copy(side, early + i, z).wait_send()

    for d in range(1, size):
        mask_copy(d).wait_send()

        @pl.when(is_end)
        def _(d=d):
            end_copy(d, 0).wait_send()

        @pl.when(is_mid)
        def _(d=d):
            mid_copy(d, 0).wait_send()

    for up in range(2):
        az_copy(up).wait_send()

    for side in range(2):

        @pl.when(me < size - 1 if side else me > 0)
        def _(side=side):
            for b in range(beams):
                tile_copy(side, b).wait_send()
            for up in range(2):
                corner_copy(up, side).wait_send()


def chain(echoes, arc_start, arc_offsets, doppler_bins, steer_angles, train_mask, early):
    columns, num_pulses, cells = echoes.shape[1:]
    num_sel = arc_offsets.shape[1]
    num_chan = doppler_bins.shape[1]
    size = lax.axis_size("rng")
    beams = BEAMS // lax.axis_size("az")
    dof = BINS * num_sel
    steps = beams // 2
    late = steps - early
    n = size // 2
    width = ARC // 2
    w = width // steps
    side_chan = num_chan // 2
    half = side_chan * dof
    items = early * side_chan
    lanes = 128
    table_re, table_im = doppler_table(num_pulses)
    table = jnp.concatenate(
        [jnp.concatenate([table_re, -table_im], 1), jnp.concatenate([table_im, table_re], 1)], 0
    )
    blocks = train_mask.shape[1]
    cell_mask = (
        jnp.broadcast_to(train_mask[:, :, None], (beams, blocks, BLK))
        .reshape(beams, blocks * BLK)
        .astype(jnp.float32)
    )
    vm = pltpu.VMEM
    dma = pltpu.SemaphoreType.DMA
    f32 = jnp.float32
    bf16 = jnp.bfloat16
    smem = pl.BlockSpec(memory_space=pltpu.SMEM)
    vmem = pl.BlockSpec(memory_space=vm)
    tile = (num_chan, cells)
    scratch = [
        vm((2, columns + 2 * width, num_pulses, cells), bf16),
        vm((steps, 2, w, num_pulses, cells), bf16),
        vm((steps, 2, w, num_pulses, cells), bf16),
        vm((beams, 2, num_pulses, num_sel, cells), bf16),
        vm((beams, 2, dof, half), f32),
        vm((steps, 2, dof, half), f32),
        vm((steps, 2, dof, half), f32),
        vm((2, early, dof, half), f32),
        vm((late, n, dof, half), f32),
        vm((early, dof, half), f32),
        vm((lanes, lanes), f32),
        vm((dof, items, dof), f32),
        vm((dof, dof, items), f32),
        vm((dof, dof + 8, items), f32),
        vm((dof, dof + 8, items), f32),
        vm((dof, items), f32),
        vm((dof, items), f32),
        vm((size, beams, cells), f32),
        vm((beams, lanes), f32),
        vm((items, lanes), bf16),
        vm((2, 2, items, lanes), bf16),
        vm((2, 2, late * side_chan, lanes), bf16),
        vm((2, 2, items, lanes), f32),
        vm((2, 2, late * side_chan, lanes), f32),
        vm((beams + 2,) + tile, f32),
        vm((beams + 2,) + tile, f32),
        vm((beams + 2,) + tile, f32),
        vm((beams + 2,) + tile, f32),
        dma,
        dma((2, steps)),
        dma((2, steps)),
        dma((steps,)),
        dma((steps,)),
        dma((2, early)),
        dma((2, early)),
        dma((late, 2)),
        dma((late, n)),
        dma((size,)),
        dma((size,)),
        dma((size,)),
        dma((2, 2)),
        dma((2, 2)),
        dma((2, beams)),
        dma((2, beams)),
        dma((2,)),
        dma((2,)),
        dma((2, 2)),
        dma((2, 2)),
    ]
    return pl.pallas_call(
        functools.partial(chain_kernel, early),
        in_specs=[smem] * 5 + [pl.BlockSpec(memory_space=pl.ANY)] + [vmem] * 3,
        out_specs=vmem,
        out_shape=jax.ShapeDtypeStruct((beams,) + tile, f32),
        scratch_shapes=scratch,
        compiler_params=pltpu.CompilerParams(
            collective_id=2, has_side_effects=True, vmem_limit_bytes=CHAIN_VMEM
        ),
        name="chain",
    )(
        arc_start,
        arc_offsets.T,
        doppler_bins.T,
        jnp.cos(steer_angles.T),
        jnp.sin(steer_angles.T),
        echoes,
        table,
        cell_mask,
        doppler_bins.T.astype(f32),
    )


EARLY_PARTS = (3, 4)


def body(echoes, arc_start, arc_offsets, doppler_bins, steer_angles, train_mask):
    columns = echoes.shape[1]
    num_pulses = echoes.shape[2]
    cells = echoes.shape[3]
    num_sel = arc_offsets.shape[1]
    chan_count = doppler_bins.shape[1]
    cycle_size = lax.axis_size("az")
    cycle_pos = lax.axis_index("az")
    rng_size = lax.axis_size("rng")
    beam_count = BEAMS // cycle_size
    item_count = beam_count * chan_count
    dof = BINS * num_sel
    pairs = beam_count // 2
    early = pairs * EARLY_PARTS[0] // EARLY_PARTS[1]
    if (
        columns == ARC
        and beam_count % 2 == 0
        and pairs * (COLS // BEAMS) == ARC // 2
        and rng_size == 8
        and cycle_size > 2
        and cells == 128
        and chan_count % 16 == 0
        and chan_count // 2 * dof % 128 == 0
        and 2 * dof + 8 <= 128
        and pairs >= 4
        and early * (chan_count // 2) <= 128
    ):
        return chain(
            echoes, arc_start, arc_offsets, doppler_bins, steer_angles, train_mask, early
        )
    table_re, table_im = doppler_table(num_pulses)
    table = jnp.concatenate(
        [jnp.concatenate([table_re, -table_im], 1), jnp.concatenate([table_im, table_re], 1)], 0
    )

    def own(x):
        return lax.dynamic_slice_in_dim(x, cycle_pos * beam_count, beam_count, axis=0)

    arc_first = (own(arc_start) - cycle_pos * columns + ARC // 2) % COLS
    col_index = arc_first[:, None] + own(arc_offsets)
    bins_own = own(doppler_bins)
    angles = own(steer_angles)
    block_count = train_mask.shape[1]
    cell_mask = (
        jnp.broadcast_to(train_mask[:, :, None], (beam_count, block_count, BLK))
        .reshape(beam_count, 1, block_count * BLK)
        .astype(jnp.bfloat16)
    )
    smem = pl.BlockSpec(memory_space=pltpu.SMEM)

    def snap_gram(extended, first, last, base):
        share = last - first
        ext_cols = extended.shape[1]
        return pl.pallas_call(
            snap_gram_kernel,
            grid=(share,),
            in_specs=[
                smem,
                smem,
                smem,
                smem,
                pl.BlockSpec((2, ext_cols, num_pulses, cells), lambda b: (0, 0, 0, 0)),
                pl.BlockSpec(table.shape, lambda b: (0, 0)),
                pl.BlockSpec((1, 1, cells), lambda b: (b, 0, 0)),
            ],
            out_specs=[
                pl.BlockSpec((1, 2, num_pulses, num_sel, cells), lambda b: (b, 0, 0, 0, 0)),
                pl.BlockSpec((1, dof, chan_count * dof), lambda b: (b, 0, 0)),
            ],
            out_shape=[
                jax.ShapeDtypeStruct((share, 2, num_pulses, num_sel, cells), jnp.bfloat16),
                jax.ShapeDtypeStruct((share, dof, chan_count * dof), jnp.float32),
            ],
            compiler_params=pltpu.CompilerParams(vmem_limit_bytes=VMEM_LIMIT),
            cost_estimate=pl.CostEstimate(
                flops=share * 600_000_000, bytes_accessed=share * 1_500_000, transcendentals=0
            ),
            name="snap_gram",
        )(
            col_index[first:last] - base,
            bins_own[first:last],
            jnp.cos(angles)[first:last],
            jnp.sin(angles)[first:last],
            extended,
            table,
            cell_mask[first:last],
        )

    width = ARC // 2
    forward = [(i, (i + 1) % cycle_size) for i in range(cycle_size)]
    backward = [(target, source) for source, target in forward]
    low = lax.ppermute(echoes[:, columns - width :], "az", forward)
    high = lax.ppermute(echoes[:, :width], "az", backward)
    step = COLS // BEAMS
    half = beam_count // 2
    if (half - 1) * step + step - 1 + ARC - 1 < width + columns and half * step >= width:
        v_lo, gram_lo = snap_gram(jnp.concatenate([low, echoes], 1), 0, half, 0)
        high, v_lo, gram_lo = lax.optimization_barrier((high, v_lo, gram_lo))
        v_hi, gram_hi = snap_gram(jnp.concatenate([echoes, high], 1), half, beam_count, width)
        v_parts = (v_lo, v_hi)
        grams = (gram_lo, gram_hi)
        if rng_size % 4 or item_count // rng_size < chan_count:
            grams = (jnp.concatenate(grams, 0),)
    else:
        v_one, gram_one = snap_gram(jnp.concatenate([low, echoes, high], 1), 0, beam_count, 0)
        v_parts = (v_one,)
        grams = (gram_one,)

    per = item_count // rng_size
    if per < chan_count:
        split = chan_count // per
        gram = grams[0].reshape(beam_count, dof, split, per * dof)
        grams = (jnp.swapaxes(gram, 1, 2).reshape(beam_count * split, dof, per * dof),)
        width = per
    else:
        width = chan_count
    vm = pltpu.VMEM
    dma = pltpu.SemaphoreType.DMA
    line = rng_size // 2
    chunk = (grams[0].shape[0] * len(grams) // rng_size, dof, grams[0].shape[2])
    part = pl.pallas_call(
        functools.partial(scatter_kernel, line, len(grams)),
        in_specs=[pl.BlockSpec(memory_space=vm)] * len(grams),
        out_specs=pl.BlockSpec(memory_space=vm),
        out_shape=jax.ShapeDtypeStruct(chunk, jnp.float32),
        scratch_shapes=[vm((line,) + chunk, jnp.float32)] * 4 + [dma((line,))] * 6,
        compiler_params=pltpu.CompilerParams(
            collective_id=0, has_side_effects=True, vmem_limit_bytes=VMEM_LIMIT
        ),
        name="scatter",
    )(*[g.reshape((rng_size // len(grams),) + chunk) for g in grams])
    solved = pl.pallas_call(
        solve_kernel,
        out_shape=jax.ShapeDtypeStruct((2 * dof + 8, per), jnp.float32),
        scratch_shapes=[
            vm((dof, per, dof), jnp.float32),
            vm((dof, dof, per), jnp.float32),
            vm((dof, dof + 8, per), jnp.float32),
            vm((dof, dof + 8, per), jnp.float32),
            vm((dof, per), jnp.float32),
            vm((dof, per), jnp.float32),
        ],
        compiler_params=pltpu.CompilerParams(vmem_limit_bytes=VMEM_LIMIT),
        name="solve",
    )(part)
    lanes = 128
    local_count = (BLK * jnp.sum(train_mask, axis=1)).astype(jnp.float32)
    pad_rows = -per % 8
    payload = jnp.concatenate(
        [
            jnp.pad(solved.T, ((0, pad_rows), (0, lanes - solved.shape[0]))),
            jnp.broadcast_to(local_count[:, None], (beam_count, lanes)),
        ],
        0,
    )
    halves = len(v_parts)
    any_spec = pl.BlockSpec(memory_space=pl.ANY)
    block = (chan_count, cells)
    out = pl.pallas_call(
        functools.partial(apply_kernel, halves, per, dof),
        in_specs=[pl.BlockSpec(memory_space=vm)] * 2 + [any_spec] * halves,
        out_specs=pl.BlockSpec(memory_space=vm),
        out_shape=jax.ShapeDtypeStruct((beam_count,) + block, jnp.float32),
        scratch_shapes=[
            vm((beam_count, 2, num_pulses, num_sel, cells), jnp.bfloat16),
            vm((rng_size,) + payload.shape, jnp.float32),
            vm((beam_count,) + block, jnp.float32),
            vm((2, 8, item_count), jnp.float32),
            vm((2, 8, item_count), jnp.float32),
            vm((beam_count,) + block, jnp.float32),
            vm(block, jnp.float32),
            vm(block, jnp.float32),
            dma((halves,)),
            dma((rng_size,)),
            dma((rng_size,)),
            dma((2,)),
            dma((2,)),
            dma((2,)),
            dma((2,)),
        ],
        compiler_params=pltpu.CompilerParams(
            collective_id=1, has_side_effects=True, vmem_limit_bytes=VMEM_LIMIT
        ),
        name="apply",
    )(payload, bins_own[:, :, None], *v_parts)
    return out


def solution(mesh):
    return jax.shard_map(
        body,
        mesh=mesh,
        in_specs=(P(None, "az", None, "rng"), P(), P(), P(), P(), P("az", "rng")),
        out_specs=P("az", None, "rng"),
        check_vma=False,
    )
```

profile of v0, /device:TPU:1, one launch (start us, length us, event | category | flops | bytes accessed | tf_op | source)
XLA Modules:
  0.0 75.7 jit_solution(15180081007703067703)
XLA Ops:
  0.0 0.0 copy-start
  0.0 0.7 convert_bitcast_fusion
  0.7 0.7 reshape.7.mask_ref
  1.3 0.0 copy-done
  1.3 0.0 copy-start.1
  1.3 0.6 bitcast_convert_fusion.chan_ref
  1.9 0.1 fusion.6
  2.0 0.0 copy-done.1
  2.0 0.6 sine_bitcast_fusion
  2.7 0.1 sine_convert_fusion
  2.8 0.7 maximum_maximum_fusion.table_ref
  3.5 70.7 %chain.1 = f32[16,16,128]{2,1,0:T(8,128)} custom-call(s32[64]{0:T(128)} %start_ref.1, s32[16,64]{1,0:T(8,128)} %bitcast.10, s32[16,64]{1,0:T(8,128)} %bitcast.9, f32[16,64]{1,0:T(8,128)} %get-tuple-element.6.cos_ref, f32[16,64]{1,0:T(8,128)} %get-tuple-element.5.sin_ref, bf16[2,64,32,128]{3,2,1,0:T(8,128)(2,1)} %echoes.1, ...), custom_call_target="tpu_custom_call" | custom-call | tf_op jit(solution)/shard_map/chain/pallas_call | solution.py:1130
  74.2 1.6 %copy.8 = f32[16,16,128]{2,1,0:T(8,128)} copy(f32[16,16,128]{2,1,0:T(8,128)} %chain.1) | data formatting | bytes 262144
Async XLA Ops:
  0.0 1.3 %copy-start = (s32[64,16]{0,1:T(8,128)S(1)}, s32[64,16]{0,1:T(8,128)}, u32[]{:S(2)}) copy-start(s32[64,16]{0,1:T(8,128)} %param.9) | copy-start | bytes 12292
  1.3 0.7 copy-start.1
where the time goes:
time: 76.4 us; the launch traced here: 75.7 us
  Pallas kernels  70.7 us (93%)
  local copies, waits for them, and re-layouts  2.91 us (4%)
  other arithmetic  2.13 us (3%)
    pallas_call x1, Pallas kernels, chain(): pl.pallas_call(functools.partial(chain_kernel, early), in_specs=[smem] *...  70.7 us
    unnamed x5, local copies, waits for them, and re-layouts  1.59 us

commit v1 on v0

--- a/solution.py
+++ b/solution.py
@@ -1,6 +1,7 @@
 import functools
 
 import jax
+import numpy as np
 import jax.numpy as jnp
 from jax import lax
 from jax.experimental import pallas as pl
@@ -16,6 +17,8 @@
 LOADING = 0.1
 VMEM_LIMIT = 48 << 20
 CHAIN_VMEM = 66_200_000
+CODE_TOP = 32000.0
+LAG = 3
 
 
 def doppler_table(num_pulses):
@@ -71,7 +74,7 @@
     gram_ref[0] = jnp.concatenate(packed, 1)
 
 
-def solve_kernel(part_ref, out_ref, stack, turned, hr, hi, xr, xi):
+def solve_kernel(part_ref, out_ref, stack, turned, hr, hi, xr, xi, yr, yi):
     lead, dof, wide = part_ref.shape
     width = wide // dof
     lanes = lead * width
@@ -105,8 +108,8 @@
                 imag = jnp.where(row < col, straight, jnp.where(row > col, -flip, 0.0))
             hr[rows, cols, :] = real
             hi[rows, cols, :] = imag
-    hr[:, dof:, :] = jnp.ones((dof, 8, lanes), jnp.float32)
-    hi[:, dof:, :] = jnp.zeros((dof, 8, lanes), jnp.float32)
+    yr[...] = jnp.ones_like(yr)
+    yi[...] = jnp.zeros_like(yi)
     xr[...] = jnp.zeros_like(xr)
     xi[...] = jnp.zeros_like(xi)
     sub = lax.broadcasted_iota(jnp.int32, (8, lanes), 0)
@@ -115,8 +118,10 @@
 
         def step(k, carry, kb=kb):
             pivot = 1.0 / hr[k, pl.ds(k, 1), :]
-            rr = [hr[k, 8 * b : 8 * b + 8, :] for b in range(kb, nb + 1)]
-            ri = [hi[k, 8 * b : 8 * b + 8, :] for b in range(kb, nb + 1)]
+            rr = [hr[k, 8 * b : 8 * b + 8, :] for b in range(kb, nb)]
+            ri = [hi[k, 8 * b : 8 * b + 8, :] for b in range(kb, nb)]
+            gr = jnp.broadcast_to(yr[pl.ds(k, 1), :], (8, lanes))
+            gi = jnp.broadcast_to(yi[pl.ds(k, 1), :], (8, lanes))
             for ib in range(kb, nb):
                 fr = rr[ib - kb] * pivot
                 fi = -ri[ib - kb] * pivot
@@ -124,11 +129,14 @@
                     live = sub + 8 * kb > k
                     fr = jnp.where(live, fr, 0.0)
                     fi = jnp.where(live, fi, 0.0)
+                own = slice(8 * ib, 8 * ib + 8)
+                yr[own, :] = yr[own, :] - (fr * gr - fi * gi)
+                yi[own, :] = yi[own, :] - (fr * gi + fi * gr)
                 for s in range(8):
                     i = 8 * ib + s
                     cr = jnp.broadcast_to(fr[s : s + 1], (8, lanes))
                     ci = jnp.broadcast_to(fi[s : s + 1], (8, lanes))
-                    for b in range(ib, nb + 1):
+                    for b in range(ib, nb):
                         pr, pi = rr[b - kb], ri[b - kb]
                         sl = slice(8 * b, 8 * b + 8)
                         hr[i, sl, :] = hr[i, sl, :] - (cr * pr - ci * pi)
@@ -150,8 +158,8 @@
                 sr = sr + (ar * br - ai * bi)
                 si = si + (ar * bi + ai * br)
             pivot = 1.0 / hr[i, pl.ds(i, 1), :]
-            top_r = hr[i, dof : dof + 1, :]
-            top_i = hi[i, dof : dof + 1, :]
+            top_r = yr[pl.ds(i, 1), :]
+            top_i = yi[pl.ds(i, 1), :]
             xr[pl.ds(i, 1), :] = (top_r - jnp.sum(sr, 0, keepdims=True)) * pivot
             xi[pl.ds(i, 1), :] = (top_i - jnp.sum(si, 0, keepdims=True)) * pivot
             return carry
@@ -457,26 +465,34 @@
 
 
 def chain_kernel(
-    early,
+    start_hbm,
+    offs_hbm,
+    bins_hbm,
+    train_hbm,
+    angle_hbm,
+    echoes,
+    table_hbm,
+    spread_hbm,
+    out_ref,
     start_ref,
     offs_ref,
     bins_ref,
-    cos_ref,
-    sin_ref,
-    echoes,
+    train_ref,
+    angle_ref,
+    chan_ref,
     table_ref,
-    mask_ref,
-    chan_ref,
-    out_ref,
+    spread_ref,
+    turn,
     ext,
     low,
     high,
     v_all,
     gram,
     pair,
-    acc,
-    ring,
-    direct,
+    coded,
+    scale,
+    code_in,
+    scale_in,
     part,
     solved,
     stack,
@@ -485,13 +501,14 @@
     hi,
     xr,
     xi,
+    yr,
+    yi,
     masks,
+    totals,
     counts,
     pay,
-    gat_e,
-    gat_l,
-    wts_e,
-    wts_l,
+    gat,
+    tiles,
     pw,
     pl_left,
     pl_right,
@@ -501,15 +518,12 @@
     hrecv,
     psend,
     precv,
-    rsend,
-    rrecv,
     dsend,
     drecv,
     msend,
     mrecv,
     gsend,
-    grecv_e,
-    grecv_l,
+    grecv,
     lsend,
     lrecv,
     tsend,
@@ -528,37 +542,60 @@
     columns = echoes.shape[1]
     pulses = echoes.shape[2]
     num_sel = offs_ref.shape[0]
+    blocks = train_ref.shape[0]
     dof = BINS * num_sel
     taps = pulses * num_sel
     steps = beams // 2
-    late = steps - early
     width = ARC // 2
     w = width // steps
     side_chan = num_chan // 2
+    half = side_chan * dof
+    lanes = pay.shape[1]
     az_next = lax.rem(az + 1, m)
     az_prev = lax.rem(az + m - 1, m)
     ahead = lax.rem(me + 1, size)
     behind = lax.rem(me + size - 1, size)
+    mate = 2 * z + 1 - c
     mid_l = n // 2 - 1
     mid_r = n // 2
-    is_end = jnp.logical_or(z == 0, z == n - 1)
+    owners = ((0, mid_l), (1, mid_r))
     is_mid = jnp.logical_or(z == mid_l, z == mid_r)
 
-    own_cols = pltpu.make_async_copy(echoes, ext.at[:, width : width + columns], esem)
-    own_cols.start()
+    loads = [
+        pltpu.make_async_copy(src, dst, esem.at[i])
+        for i, (src, dst) in enumerate(
+            (
+                (start_hbm, start_ref),
+                (offs_hbm, offs_ref),
+                (bins_hbm, bins_ref),
+                (train_hbm, train_ref),
+                (angle_hbm, angle_ref),
+                (bins_hbm, chan_ref),
+                (table_hbm, table_ref),
+                (spread_hbm, spread_ref),
+                (echoes, ext.at[:, width : width + columns]),
+            )
+        )
+    ]
+    barrier = pltpu.get_barrier_semaphore()
+    for other in (az_next, az_prev):
+        pl.semaphore_signal(barrier, inc=1, device_id={"az": other}, device_id_type=MESH)
+    pl.semaphore_signal(barrier, inc=1, device_id={"rng": mate}, device_id_type=MESH)
+    for place in range(n):
+        near = jnp.logical_or(is_mid, place in (mid_l, mid_r))
+
+        @pl.when(jnp.logical_and(z != place, near))
+        def _(place=place):
+            pl.semaphore_signal(
+                barrier, inc=1, device_id={"rng": 2 * place + c}, device_id_type=MESH
+            )
+
+    for load in loads:
+        load.start()
     pl_left[...] = jnp.zeros(pl_left.shape, jnp.float32)
     pl_right[...] = jnp.zeros(pl_right.shape, jnp.float32)
-    barrier = pltpu.get_barrier_semaphore()
-    for d in range(1, size):
-        peer = lax.rem(me + d, size)
-        pl.semaphore_signal(barrier, inc=1, device_id={"rng": peer}, device_id_type=MESH)
-    for other in (az_next, az_prev):
-        pl.semaphore_signal(barrier, inc=1, device_id={"az": other}, device_id_type=MESH)
-        for r in (ahead, behind):
-            pl.semaphore_signal(
-                barrier, inc=1, device_id={"az": other, "rng": r}, device_id_type=MESH
-            )
-    pl.semaphore_wait(barrier, size + 5)
+    solved[...] = jnp.zeros(solved.shape, jnp.float32)
+    pl.semaphore_wait(barrier, 3 + jnp.where(is_mid, n - 1, 2))
 
     def low_copy(i):
         return pltpu.make_async_remote_copy(
@@ -583,24 +620,31 @@
     for i in range(steps):
         low_copy(i).start()
         high_copy(i).start()
-
-    def mask_copy(d):
-        return pltpu.make_async_remote_copy(
-            src_ref=mask_ref,
-            dst_ref=masks.at[me],
-            send_sem=msend.at[d],
-            recv_sem=mrecv.at[me],
-            device_id={"rng": lax.rem(me + d, size)},
-            device_id_type=MESH,
-        )
-
-    for d in range(1, size):
-        mask_copy(d).start()
-    masks[me] = mask_ref[...]
-
-    part[...] = jnp.zeros(part.shape, jnp.float32)
-    solved[...] = jnp.zeros(solved.shape, jnp.float32)
-    own_cols.wait()
+    for load in loads:
+        load.wait()
+
+    cell = lax.broadcasted_iota(jnp.int32, (1, cells), 1) // BLK
+    for b in range(beams):
+        row = jnp.zeros((1, cells), jnp.float32)
+        for blk in range(blocks):
+            row = jnp.where(cell == blk, train_ref[blk, b].astype(jnp.float32), row)
+        masks[0, b : b + 1, :] = row
+
+    mask_copy = pltpu.make_async_remote_copy(
+        src_ref=masks.at[0],
+        dst_ref=masks.at[1],
+        send_sem=msend,
+        recv_sem=mrecv,
+        device_id={"rng": mate},
+        device_id_type=MESH,
+    )
+    mask_copy.start()
+    turn[0] = jnp.cos(angle_ref[...])
+    turn[1] = jnp.sin(angle_ref[...])
+    mask_copy.wait_recv()
+    totals[...] = jnp.broadcast_to(
+        jnp.sum(masks[0] + masks[1], 1, keepdims=True), totals.shape
+    )
 
     def mine(t):
         return jnp.where(c == 0, steps - 1 - t, steps + t)
@@ -611,53 +655,48 @@
             dst_ref=pair.at[t],
             send_sem=psend.at[t],
             recv_sem=precv.at[t],
-            device_id={"rng": 2 * z + 1 - c},
+            device_id={"rng": mate},
             device_id_type=MESH,
         )
 
-    def ring_copy(side, t):
-        target = lax.rem(me + 2, size) if side else lax.rem(me + size - 2, size)
-        return pltpu.make_async_remote_copy(
-            src_ref=acc.at[t, side],
-            dst_ref=ring.at[side, t],
-            send_sem=rsend.at[side, t],
-            recv_sem=rrecv.at[side, t],
-            device_id={"rng": target},
-            device_id_type=MESH,
-        )
-
-    def direct_copy(side, t, source):
+    def code_copies(side, t, source):
         owner = 2 * (mid_r if side else mid_l) + c
-        return pltpu.make_async_remote_copy(
-            src_ref=acc.at[t, side],
-            dst_ref=direct.at[t - early, source],
-            send_sem=dsend.at[t - early, side],
-            recv_sem=drecv.at[t - early, source],
-            device_id={"rng": owner},
-            device_id_type=MESH,
-        )
+        return [
+            pltpu.make_async_remote_copy(
+                src_ref=src.at[t, side],
+                dst_ref=dst.at[t, source],
+                send_sem=dsend.at[i, t, side],
+                recv_sem=drecv.at[i, t, source],
+                device_id={"rng": owner},
+                device_id_type=MESH,
+            )
+            for i, (src, dst) in enumerate(((coded, code_in), (scale, scale_in)))
+        ]
 
     table = table_ref[...]
+    blane = lax.broadcasted_iota(jnp.int32, angle_ref.shape, 1)
 
     def one_beam(b):
         bg = az * beams + b
         first = lax.rem(start_ref[bg] - az * columns + (width + COLS), COLS)
         first = jnp.minimum(first, ext.shape[1] - ARC)
+        here = blane == bg
+        cosine = jnp.sum(jnp.where(here, turn[0], 0.0), 1, keepdims=True)
+        sine = jnp.sum(jnp.where(here, turn[1], 0.0), 1, keepdims=True)
+        cosine = jnp.broadcast_to(cosine, (num_sel, cells))[None]
+        sine = jnp.broadcast_to(sine, (num_sel, cells))[None]
         parts_re, parts_im = [], []
         for j in range(num_sel):
             col = first + offs_ref[j, bg]
             data = jnp.concatenate([ext[0, col], ext[1, col]], axis=0)
             spec = jnp.dot(table, data, preferred_element_type=jnp.float32)
-            cosine = cos_ref[j, bg]
-            sine = sin_ref[j, bg]
-            spec_re = spec[:pulses]
-            spec_im = spec[pulses:]
-            parts_re.append(cosine * spec_re - sine * spec_im)
-            parts_im.append(sine * spec_re + cosine * spec_im)
-        for p, pieces in enumerate((parts_re, parts_im)):
-            stacked = jnp.swapaxes(jnp.stack(pieces, 0), 0, 1)
-            v_all[b, p] = stacked.astype(jnp.bfloat16)
-        mask_row = mask_ref[pl.ds(b, 1), :].astype(jnp.bfloat16)
+            parts_re.append(spec[:pulses])
+            parts_im.append(spec[pulses:])
+        spec_re = jnp.swapaxes(jnp.stack(parts_re, 0), 0, 1)
+        spec_im = jnp.swapaxes(jnp.stack(parts_im, 0), 0, 1)
+        v_all[b, 0] = (cosine * spec_re - sine * spec_im).astype(jnp.bfloat16)
+        v_all[b, 1] = (sine * spec_re + cosine * spec_im).astype(jnp.bfloat16)
+        mask_row = masks[0, pl.ds(b, 1), :].astype(jnp.bfloat16)
         bins = [bins_ref[k, bg] for k in range(num_chan)]
         packed = gram_of(v_all, b, bins, mask_row)
         gram[b, 0] = jnp.concatenate(packed[:side_chan], 1)
@@ -670,13 +709,7 @@
             high_copy(s).wait_recv()
             ext[:, pl.ds(width - w * (s + 1), w)] = low[s]
             ext[:, pl.ds(width + columns + w * s, w)] = high[s]
-
-            def two(i, carry):
-                one_beam(jnp.where(i == 0, steps - 1 - s, steps + s))
-                return carry
-
-            lax.fori_loop(0, 2, two, 0)
-            pair_copy(s).start()
+            one_beam(steps - 1 - s)
 
         t = s - 1
 
@@ -684,135 +717,94 @@
         def _():
             pair_copy(t).wait_recv()
             own = mine(t)
-            acc[t] = gram[own] + pair[t]
-
-            @pl.when(t < early)
-            def _():
-                @pl.when(z == 0)
-                def _():
-                    ring_copy(1, t).start()
-
-                @pl.when(z == n - 1)
-                def _():
-                    ring_copy(0, t).start()
-
-            @pl.when(t >= early)
-            def _():
-                for side, owner in ((0, mid_l), (1, mid_r)):
-
-                    @pl.when(z != owner)
-                    def _(side=side):
-                        direct_copy(side, t, z).start()
-
-        for side in range(2):
-            place = z if side else n - 1 - z
-            tt = s - 1 - place
-
-            @pl.when(jnp.logical_and(place > 0, jnp.logical_and(tt >= 0, tt < early)))
-            def _(side=side, place=place, tt=tt):
-                ring_copy(side, tt).wait_recv()
-                total = acc[tt, side] + ring[side, tt]
-
-                @pl.when(place < n - 1)
-                def _():
-                    acc[tt, side] = total
-                    ring_copy(side, tt).start()
-
-                @pl.when(place == n - 1)
-                def _():
+            number = totals[pl.ds(own, 1), :]
+            for side, owner in owners:
+                total = gram[own, side] + pair[t, side]
+
+                @pl.when(z == owner)
+                def _(side=side, total=total):
+                    part[t] = total
+                    counts[t] = number
+
+                @pl.when(z != owner)
+                def _(side=side, total=total):
+                    top = jnp.max(jnp.abs(total), 0, keepdims=True)
+                    top = jnp.maximum(top, 1e-30)
+                    code = jnp.round(total * (CODE_TOP / top))
+                    coded[t, side] = code.astype(jnp.int32).astype(jnp.int16)
+                    scale[t, side, :, :half] = top * (1.0 / CODE_TOP)
+                    scale[t, side, :, half:] = number
+                    for copy in code_copies(side, t, z):
+                        copy.start()
+
+        tt = s - LAG
+
+        @pl.when(jnp.logical_and(tt >= 0, tt < steps))
+        def _():
+            for side, owner in owners:
+
+                @pl.when(z == owner)
+                def _(side=side, owner=owner):
+                    total = part[tt]
+                    number = counts[tt]
+                    for source in range(n):
+                        if source != owner:
+                            for copy in code_copies(side, tt, source):
+                                copy.wait_recv()
+                            code = code_in[tt, source].astype(jnp.int32).astype(jnp.float32)
+                            total = total + code * scale_in[tt, source, :, :half]
+                            number = number + scale_in[tt, source, :, half:]
                     part[tt] = total
+                    counts[tt] = number
+
+        @pl.when(s < steps)
+        def _():
+            one_beam(steps + s)
+            pair_copy(s).start()
 
         return carry
 
-    lax.fori_loop(0, max(steps + 1, early + n), slot, 0)
-
-    for side, owner in ((0, mid_l), (1, mid_r)):
-
-        @pl.when(z == owner)
-        def _(side=side, owner=owner):
-            for i in range(late):
-                total = acc[early + i, side]
-                for source in range(n):
-                    if source != owner:
-                        direct_copy(side, early + i, source).wait_recv()
-                        total = total + direct[i, source]
-                part[i] = total
-
-    for d in range(1, size):
-        src = lax.rem(me + d, size)
-        pltpu.make_async_remote_copy(
-            src_ref=mask_ref,
-            dst_ref=masks.at[src],
-            send_sem=msend.at[d],
-            recv_sem=mrecv.at[src],
-            device_id={"rng": src},
-            device_id_type=MESH,
-        ).wait_recv()
-    all_masks = masks[0]
-    for r in range(1, size):
-        all_masks = all_masks + masks[r]
-    counts[...] = jnp.broadcast_to(jnp.sum(all_masks, 1, keepdims=True), counts.shape)
-
-    solve_kernel(part, solved, stack, turned, hr, hi, xr, xi)
-    lanes = pay.shape[1]
-    flipped = solved[...].T
-    items = early * side_chan
-    scaled = []
-    for t in range(early):
-        tt = jnp.where(is_mid, early + jnp.minimum(t, late - 1), t)
-        scaled.append(
-            flipped[side_chan * t : side_chan * (t + 1)] * counts[pl.ds(mine(tt), 1), :]
-        )
-    full = jnp.concatenate(scaled, 0)
-    lane = lax.broadcasted_iota(jnp.int32, (items, lanes), 1)
-    hi_part = full.astype(jnp.bfloat16).astype(jnp.float32)
-    rest = full - hi_part
-    mid_part = rest.astype(jnp.bfloat16).astype(jnp.float32)
-    lo_part = rest - mid_part
-    coded = jnp.where(
-        lane == 2 * dof + 1, mid_part, jnp.where(lane == 2 * dof + 2, lo_part, hi_part)
-    )
-    pay[...] = coded.astype(jnp.bfloat16)
-
-    def end_copy(d, side):
+    lax.fori_loop(0, steps + LAG, slot, 0)
+
+    items = steps * side_chan
+
+    def send_copy(d, side):
         return pltpu.make_async_remote_copy(
             src_ref=pay,
-            dst_ref=gat_e.at[side, c],
+            dst_ref=gat.at[side, c],
             send_sem=gsend.at[d],
-            recv_sem=grecv_e.at[side, c],
+            recv_sem=grecv.at[side, c],
             device_id={"rng": lax.rem(me + d, size)},
             device_id_type=MESH,
         )
 
-    def mid_copy(d, side):
-        return pltpu.make_async_remote_copy(
-            src_ref=pay.at[: late * side_chan],
-            dst_ref=gat_l.at[side, c],
-            send_sem=gsend.at[d],
-            recv_sem=grecv_l.at[side, c],
-            device_id={"rng": lax.rem(me + d, size)},
-            device_id_type=MESH,
-        )
-
-    for side, owner in ((0, 0), (1, n - 1)):
-
-        @pl.when(z == owner)
-        def _(side=side):
-            for d in range(1, size):
-                end_copy(d, side).start()
-            gat_e[side, c] = pay[...]
-
-    for side, owner in ((0, mid_l), (1, mid_r)):
-
-        @pl.when(z == owner)
-        def _(side=side):
-            for d in range(1, size):
-                mid_copy(d, side).start()
-            gat_l[side, c] = pay[: late * side_chan]
+    @pl.when(is_mid)
+    def _():
+        solve_kernel(part, solved, stack, turned, hr, hi, xr, xi, yr, yi)
+        flipped = solved[...].T
+        scaled = []
+        for t in range(steps):
+            scaled.append(flipped[side_chan * t : side_chan * (t + 1)] * counts[t])
+        full = jnp.concatenate(scaled, 0)
+        lane = lax.broadcasted_iota(jnp.int32, (items, lanes), 1)
+        hi_part = full.astype(jnp.bfloat16).astype(jnp.float32)
+        rest = full - hi_part
+        mid_part = rest.astype(jnp.bfloat16).astype(jnp.float32)
+        lo_part = rest - mid_part
+        split = jnp.where(
+            lane == 2 * dof + 1, mid_part, jnp.where(lane == 2 * dof + 2, lo_part, hi_part)
+        )
+        pay[...] = split.astype(jnp.bfloat16)
+        for side, owner in owners:
+
+            @pl.when(z == owner)
+            def _(side=side):
+                for d in range(1, size):
+                    send_copy(d, side).start()
+                gat[side, c] = pay[...]
 
     freq = (lax.broadcasted_iota(jnp.int32, (num_chan, taps), 1) // num_sel).astype(jnp.float32)
-    blane = lax.broadcasted_iota(jnp.int32, chan_ref.shape, 1)
-    wlane = lax.broadcasted_iota(jnp.int32, (num_chan, lanes), 1)
+    centres = chan_ref[...].astype(jnp.float32)
 
     def tile_copy(side, b):
         target = ahead if side else behind
@@ -850,12 +842,13 @@
             device_id_type=MESH,
         )
 
-    def one_power(b, wt):
-        quiet = wt[:, 2 * dof : 2 * dof + 1]
-        quiet = quiet + wt[:, 2 * dof + 1 : 2 * dof + 2] + wt[:, 2 * dof + 2 : 2 * dof + 3]
-        centre = jnp.sum(
-            jnp.where(blane == az * beams + b, chan_ref[...], 0.0), 1, keepdims=True
-        )
+    def one_power(b, t, core):
+        start = pl.multiple_of(t * side_chan, side_chan)
+        both = [tiles[side, core, pl.ds(start, side_chan), :] for side in range(2)]
+        wide = jnp.concatenate(both, 0)
+        tail = wide[:, 2 * BINS * lanes :]
+        quiet = tail[:, :1] + tail[:, 1:2] + tail[:, 2:3]
+        centre = jnp.sum(jnp.where(blane == az * beams + b, centres, 0.0), 1, keepdims=True)
         hits = []
         for q in range(BINS):
             f = centre + (q - BINS // 2)
@@ -865,13 +858,8 @@
         for p in range(2):
             plane = jnp.zeros((num_chan, taps), jnp.float32)
             for q in range(BINS):
-                start = p * dof + q * num_sel
-                piece = pltpu.roll(wt, (lanes - start) % lanes, 1) if start else wt
-                piece = jnp.where(wlane < num_sel, piece, 0.0)
-                span = num_sel
-                while span < lanes:
-                    piece = piece + pltpu.roll(piece, span, 1)
-                    span *= 2
+                at = (p * BINS + q) * lanes
+                piece = wide[:, at : at + lanes]
                 tiled = jnp.concatenate([piece] * (taps // lanes), 1)
                 plane = jnp.where(hits[q], tiled, plane)
             planes.append(plane)
@@ -892,76 +880,44 @@
         def _():
             tile_copy(0, b).start()
 
-    def gathered(sem, buf, side, owner, copy):
+    for side, owner in owners:
         for core in range(2):
 
             @pl.when(me != 2 * owner + core)
-            def _(core=core):
+            def _(side=side, core=core):
                 pltpu.make_async_remote_copy(
-                    src_ref=copy,
-                    dst_ref=buf.at[side, core],
+                    src_ref=pay,
+                    dst_ref=gat.at[side, core],
                     send_sem=gsend.at[0],
-                    recv_sem=sem.at[side, core],
+                    recv_sem=grecv.at[side, core],
                     device_id={"rng": ahead},
                     device_id_type=MESH,
                 ).wait_recv()
 
-    gathered(grecv_e, gat_e, 0, 0, pay)
-    gathered(grecv_e, gat_e, 1, n - 1, pay)
-    wts_e[...] = gat_e[...].astype(jnp.float32)
-
-    def weights(buf, i, core):
-        start = pl.multiple_of(i * side_chan, side_chan)
-        return jnp.concatenate(
-            [buf[0, core, pl.ds(start, side_chan), :], buf[1, core, pl.ds(start, side_chan), :]], 0
-        )
-
-    def early_power(i, carry):
-        t = i // 2
-        core = lax.rem(i, 2)
-        one_power(jnp.where(core == 0, steps - 1 - t, steps + t), weights(wts_e, t, core))
-        return carry
-
-    lax.fori_loop(0, 2 * early, early_power, 0)
-    short = pay.at[: late * side_chan]
-    gathered(grecv_l, gat_l, 0, mid_l, short)
-    gathered(grecv_l, gat_l, 1, mid_r, short)
-    wts_l[...] = gat_l[...].astype(jnp.float32)
-
-    def late_power(i, carry):
-        t = late - 1 - i // 2
-        core = lax.rem(i, 2)
-        one_power(
-            jnp.where(core == 0, late - 1 - t, steps + early + t), weights(wts_l, t, core)
-        )
+            tiles[side, core] = jnp.dot(
+                gat[side, core], spread_ref[...], preferred_element_type=jnp.float32
+            )
+
+    def power(i, carry):
+        one_power(i, steps - 1 - i, 0)
+        one_power(beams - 1 - i, steps - 1 - i, 1)
 
         @pl.when(i == 0)
         def _():
-            az_copy(0).start()
-
-            @pl.when(me < size - 1)
-            def _():
-                corner_copy(0, 1).start()
-
-            @pl.when(me > 0)
-            def _():
-                corner_copy(0, 0).start()
-
-        @pl.when(i == 1)
-        def _():
-            az_copy(1).start()
-
-            @pl.when(me < size - 1)
-            def _():
-                corner_copy(1, 1).start()
-
-            @pl.when(me > 0)
-            def _():
-                corner_copy(1, 0).start()
+            for up in range(2):
+                az_copy(up).start()
+
+                @pl.when(me < size - 1)
+                def _(up=up):
+                    corner_copy(up, 1).start()
+
+                @pl.when(me > 0)
+                def _(up=up):
+                    corner_copy(up, 0).start()
 
         return carry
 
-    lax.fori_loop(0, 2 * late, late_power, 0)
+    lax.fori_loop(0, steps, power, 0)
 
     lane = lax.broadcasted_iota(jnp.int32, (num_chan, cells), 1)
 
@@ -1003,33 +959,19 @@
         low_copy(i).wait_send()
         high_copy(i).wait_send()
         pair_copy(i).wait_send()
-    for i in range(early):
-
-        @pl.when(z < n - 1)
-        def _(i=i):
-            ring_copy(1, i).wait_send()
-
-        @pl.when(z > 0)
-        def _(i=i):
-            ring_copy(0, i).wait_send()
-
-    for i in range(late):
-        for side, owner in ((0, mid_l), (1, mid_r)):
+        for side, owner in owners:
 
             @pl.when(z != owner)
             def _(side=side, i=i):
-                direct_copy(side, early + i, z).wait_send()
-
-    for d in range(1, size):
-        mask_copy(d).wait_send()
-
-        @pl.when(is_end)
-        def _(d=d):
-            end_copy(d, 0).wait_send()
-
-        @pl.when(is_mid)
-        def _(d=d):
-            mid_copy(d, 0).wait_send()
+                for copy in code_copies(side, i, z):
+                    copy.wait_send()
+
+    mask_copy.wait_send()
+
+    @pl.when(is_mid)
+    def _():
+        for d in range(1, size):
+            send_copy(d, 0).wait_send()
 
     for up in range(2):
         az_copy(up).wait_send()
@@ -1044,7 +986,7 @@
                 corner_copy(up, side).wait_send()
 
 
-def chain(echoes, arc_start, arc_offsets, doppler_bins, steer_angles, train_mask, early):
+def chain(echoes, arc_start, arc_offsets, doppler_bins, steer_angles, train_mask):
     columns, num_pulses, cells = echoes.shape[1:]
     num_sel = arc_offsets.shape[1]
     num_chan = doppler_bins.shape[1]
@@ -1052,73 +994,81 @@
     beams = BEAMS // lax.axis_size("az")
     dof = BINS * num_sel
     steps = beams // 2
-    late = steps - early
     n = size // 2
     width = ARC // 2
     w = width // steps
     side_chan = num_chan // 2
     half = side_chan * dof
-    items = early * side_chan
+    items = steps * side_chan
     lanes = 128
-    table_re, table_im = doppler_table(num_pulses)
-    table = jnp.concatenate(
-        [jnp.concatenate([table_re, -table_im], 1), jnp.concatenate([table_im, table_re], 1)], 0
+    with jax.ensure_compile_time_eval():
+        table_re, table_im = doppler_table(num_pulses)
+        table = np.block([[table_re, -table_im], [table_im, table_re]])
+    source = np.arange(lanes)[:, None]
+    target = np.arange((2 * BINS + 1) * lanes)[None, :]
+    block, place = target // lanes, target % lanes
+    wanted = np.where(
+        block < 2 * BINS, block * num_sel + place % num_sel, 2 * dof + np.minimum(place, 3)
     )
-    blocks = train_mask.shape[1]
-    cell_mask = (
-        jnp.broadcast_to(train_mask[:, :, None], (beams, blocks, BLK))
-        .reshape(beams, blocks * BLK)
-        .astype(jnp.float32)
-    )
+    spread = jnp.asarray(source == wanted, jnp.bfloat16)
     vm = pltpu.VMEM
+    sm = pltpu.SMEM
     dma = pltpu.SemaphoreType.DMA
     f32 = jnp.float32
     bf16 = jnp.bfloat16
-    smem = pl.BlockSpec(memory_space=pltpu.SMEM)
-    vmem = pl.BlockSpec(memory_space=vm)
+    i32 = jnp.int32
+    i16 = jnp.int16
     tile = (num_chan, cells)
     scratch = [
+        sm(arc_start.shape, i32),
+        sm(arc_offsets.T.shape, i32),
+        sm(doppler_bins.T.shape, i32),
+        sm(train_mask.T.shape, i32),
+        vm(steer_angles.T.shape, f32),
+        vm(doppler_bins.T.shape, i32),
+        vm(table.shape, bf16),
+        vm(spread.shape, bf16),
+        vm((2,) + steer_angles.T.shape, f32),
         vm((2, columns + 2 * width, num_pulses, cells), bf16),
         vm((steps, 2, w, num_pulses, cells), bf16),
         vm((steps, 2, w, num_pulses, cells), bf16),
         vm((beams, 2, num_pulses, num_sel, cells), bf16),
         vm((beams, 2, dof, half), f32),
         vm((steps, 2, dof, half), f32),
-        vm((steps, 2, dof, half), f32),
-        vm((2, early, dof, half), f32),
-        vm((late, n, dof, half), f32),
-        vm((early, dof, half), f32),
+        vm((steps, 2, dof, half), i16),
+        vm((steps, 2, 1, half + lanes), f32),
+        vm((steps, n, dof, half), i16),
+        vm((steps, n, 1, half + lanes), f32),
+        vm((steps, dof, half), f32),
         vm((lanes, lanes), f32),
         vm((dof, items, dof), f32),
         vm((dof, dof, items), f32),
-        vm((dof, dof + 8, items), f32),
-        vm((dof, dof + 8, items), f32),
+        vm((dof, dof, items), f32),
+        vm((dof, dof, items), f32),
         vm((dof, items), f32),
         vm((dof, items), f32),
-        vm((size, beams, cells), f32),
+        vm((dof, items), f32),
+        vm((dof, items), f32),
+        vm((2, beams, cells), f32),
         vm((beams, lanes), f32),
+        vm((steps, 1, lanes), f32),
         vm((items, lanes), bf16),
         vm((2, 2, items, lanes), bf16),
-        vm((2, 2, late * side_chan, lanes), bf16),
-        vm((2, 2, items, lanes), f32),
-        vm((2, 2, late * side_chan, lanes), f32),
+        vm((2, 2, items, spread.shape[1]), f32),
         vm((beams + 2,) + tile, f32),
         vm((beams + 2,) + tile, f32),
         vm((beams + 2,) + tile, f32),
         vm((beams + 2,) + tile, f32),
-        dma,
+        dma((9,)),
         dma((2, steps)),
         dma((2, steps)),
         dma((steps,)),
         dma((steps,)),
-        dma((2, early)),
-        dma((2, early)),
-        dma((late, 2)),
-        dma((late, n)),
+        dma((2, steps, 2)),
+        dma((2, steps, n)),
+        dma,
+        dma,
         dma((size,)),
-        dma((size,)),
-        dma((size,)),
-        dma((2, 2)),
         dma((2, 2)),
         dma((2, beams)),
         dma((2, beams)),
@@ -1128,9 +1078,9 @@
         dma((2, 2)),
     ]
     return pl.pallas_call(
-        functools.partial(chain_kernel, early),
-        in_specs=[smem] * 5 + [pl.BlockSpec(memory_space=pl.ANY)] + [vmem] * 3,
-        out_specs=vmem,
+        chain_kernel,
+        in_specs=[pl.BlockSpec(memory_space=pl.ANY)] * 8,
+        out_specs=pl.BlockSpec(memory_space=vm),
         out_shape=jax.ShapeDtypeStruct((beams,) + tile, f32),
         scratch_shapes=scratch,
         compiler_params=pltpu.CompilerParams(
@@ -1141,16 +1091,12 @@
         arc_start,
         arc_offsets.T,
         doppler_bins.T,
-        jnp.cos(steer_angles.T),
-        jnp.sin(steer_angles.T),
+        train_mask.T,
+        steer_angles.T,
         echoes,
-        table,
-        cell_mask,
-        doppler_bins.T.astype(f32),
+        jnp.asarray(table),
+        spread,
     )
-
-
-EARLY_PARTS = (3, 4)
 
 
 def body(echoes, arc_start, arc_offsets, doppler_bins, steer_angles, train_mask):
@@ -1166,7 +1112,6 @@
     item_count = beam_count * chan_count
     dof = BINS * num_sel
     pairs = beam_count // 2
-    early = pairs * EARLY_PARTS[0] // EARLY_PARTS[1]
     if (
         columns == ARC
         and beam_count % 2 == 0
@@ -1177,12 +1122,10 @@
         and chan_count % 16 == 0
         and chan_count // 2 * dof % 128 == 0
         and 2 * dof + 8 <= 128
-        and pairs >= 4
-        and early * (chan_count // 2) <= 128
+        and dof % 16 == 0
+        and pairs * (chan_count // 2) <= 128
     ):
-        return chain(
-            echoes, arc_start, arc_offsets, doppler_bins, steer_angles, train_mask, early
-        )
+        return chain(echoes, arc_start, arc_offsets, doppler_bins, steer_angles, train_mask)
     table_re, table_im = doppler_table(num_pulses)
     table = jnp.concatenate(
         [jnp.concatenate([table_re, -table_im], 1), jnp.concatenate([table_im, table_re], 1)], 0
@@ -1290,8 +1233,10 @@
         scratch_shapes=[
             vm((dof, per, dof), jnp.float32),
             vm((dof, dof, per), jnp.float32),
-            vm((dof, dof + 8, per), jnp.float32),
-            vm((dof, dof + 8, per), jnp.float32),
+            vm((dof, dof, per), jnp.float32),
+            vm((dof, dof, per), jnp.float32),
+            vm((dof, per), jnp.float32),
+            vm((dof, per), jnp.float32),
             vm((dof, per), jnp.float32),
             vm((dof, per), jnp.float32),
         ],

time: 76.4 us -> 57.6 us (0.75)
  Pallas kernels: 70.7 us -> 55.8 us
  other arithmetic: 2.13 us -> 0 us
  local copies, waits for them, and re-layouts: 2.91 us -> 1.57 us
    pallas_call x1, Pallas kernels: 70.7 us -> 55.8 us  [chain(): pl.pallas_call(chain_kernel, in_specs=[pl.BlockSpec(memory_space=pl.ANY)]...]
    convert_element_type x3 -> x0, other arithmetic: 1.35 us -> none  [the longest x1 0.67 us: chain(): cell_mask = jnp.broadcast_to(train_mask[:, :, None], (beams, blocks, BLK)...]
    unnamed x5 -> x1, local copies, waits for them, and re-layouts: 1.59 us -> 1.57 us
where the time goes in v1:
time: 57.6 us; the launch traced here: 57.4 us
  Pallas kernels  55.8 us (97%)
  local copies, waits for them, and re-layouts  1.57 us (3%)
    pallas_call x1, Pallas kernels, chain(): pl.pallas_call(chain_kernel, in_specs=[pl.BlockSpec(memory_space=pl.ANY)]...  55.8 us
    unnamed x1, local copies, waits for them, and re-layouts  1.57 us

profile of v1, /device:TPU:1, one launch (start us, length us, event | category | flops | bytes accessed | tf_op | source)
XLA Modules:
  0.0 57.4 jit_solution(813672954162499295)
XLA Ops:
  0.0 55.8 %chain.1 = f32[16,16,128]{2,1,0:T(8,128)} custom-call(s32[64]{0:T(128)} %start_hbm.1, s32[16,64]{1,0:T(8,128)} %bitcast.4, s32[16,64]{1,0:T(8,128)} %bitcast.5, s32[1,16]{1,0:T(1,128)} %bitcast.7, f32[16,64]{1,0:T(8,128)} %bitcast.6, bf16[2,64,32,128]{3,2,1,0:T(8,128)(2,1)} %echoes.1, bf16[64,64]{1,0:T(8,128)(2,1)} %constant.5.clone.table_hbm, ...), custom_call_target="tpu_custom_call" | custom-call | tf_op jit(solution)/shard_map/chain/pallas_call | solution.py:1080
  55.8 1.6 %copy.10 = f32[16,16,128]{2,1,0:T(8,128)} copy(f32[16,16,128]{2,1,0:T(8,128)} %chain.1) | data formatting | bytes 262144

commit v2 on v1

--- a/solution.py
+++ b/solution.py
@@ -19,6 +19,7 @@
 CHAIN_VMEM = 66_200_000
 CODE_TOP = 32000.0
 LAG = 3
+LATE = 2
 
 
 def doppler_table(num_pulses):
@@ -465,6 +466,7 @@
 
 
 def chain_kernel(
+    early,
     start_hbm,
     offs_hbm,
     bins_hbm,
@@ -507,8 +509,10 @@
     totals,
     counts,
     pay,
-    gat,
-    tiles,
+    gat_e,
+    gat_l,
+    tiles_e,
+    tiles_l,
     pw,
     pl_left,
     pl_right,
@@ -524,6 +528,7 @@
     mrecv,
     gsend,
     grecv,
+    hello,
     lsend,
     lrecv,
     tsend,
@@ -558,7 +563,9 @@
     mate = 2 * z + 1 - c
     mid_l = n // 2 - 1
     mid_r = n // 2
-    owners = ((0, mid_l), (1, mid_r))
+    late = steps - early
+    middles = ((0, mid_l), (1, mid_r))
+    ends = ((0, 0), (1, n - 1))
     is_mid = jnp.logical_or(z == mid_l, z == mid_r)
 
     loads = [
@@ -595,6 +602,7 @@
     pl_left[...] = jnp.zeros(pl_left.shape, jnp.float32)
     pl_right[...] = jnp.zeros(pl_right.shape, jnp.float32)
     solved[...] = jnp.zeros(solved.shape, jnp.float32)
+    part[...] = jnp.zeros(part.shape, jnp.float32)
     pl.semaphore_wait(barrier, 3 + jnp.where(is_mid, n - 1, 2))
 
     def low_copy(i):
@@ -620,6 +628,13 @@
     for i in range(steps):
         low_copy(i).start()
         high_copy(i).start()
+    for side, middle in middles:
+
+        @pl.when(z == middle)
+        def _(side=side):
+            end = 2 * (n - 1 if side else 0) + c
+            pl.semaphore_signal(hello, inc=1, device_id={"rng": end}, device_id_type=MESH)
+
     for load in loads:
         load.wait()
 
@@ -649,9 +664,16 @@
     def mine(t):
         return jnp.where(c == 0, steps - 1 - t, steps + t)
 
+    def theirs(t):
+        return jnp.where(c == 0, steps + t, steps - 1 - t)
+
+    def owner_of(side, t):
+        far, near = (n - 1, mid_r) if side else (0, mid_l)
+        return jnp.where(t < early, far, near)
+
     def pair_copy(t):
         return pltpu.make_async_remote_copy(
-            src_ref=gram.at[jnp.where(c == 0, steps + t, steps - 1 - t)],
+            src_ref=gram.at[theirs(t)],
             dst_ref=pair.at[t],
             send_sem=psend.at[t],
             recv_sem=precv.at[t],
@@ -660,7 +682,7 @@
         )
 
     def code_copies(side, t, source):
-        owner = 2 * (mid_r if side else mid_l) + c
+        owner = 2 * owner_of(side, t) + c
         return [
             pltpu.make_async_remote_copy(
                 src_ref=src.at[t, side],
@@ -709,7 +731,8 @@
             high_copy(s).wait_recv()
             ext[:, pl.ds(width - w * (s + 1), w)] = low[s]
             ext[:, pl.ds(width + columns + w * s, w)] = high[s]
-            one_beam(steps - 1 - s)
+            one_beam(theirs(s))
+            pair_copy(s).start()
 
         t = s - 1
 
@@ -718,13 +741,15 @@
             pair_copy(t).wait_recv()
             own = mine(t)
             number = totals[pl.ds(own, 1), :]
-            for side, owner in owners:
+            row = jnp.where(t < early, t, t - early)
+            for side in range(2):
                 total = gram[own, side] + pair[t, side]
+                owner = owner_of(side, t)
 
                 @pl.when(z == owner)
-                def _(side=side, total=total):
-                    part[t] = total
-                    counts[t] = number
+                def _(total=total):
+                    part[row] = total
+                    counts[row] = number
 
                 @pl.when(z != owner)
                 def _(side=side, total=total):
@@ -741,67 +766,73 @@
 
         @pl.when(jnp.logical_and(tt >= 0, tt < steps))
         def _():
-            for side, owner in owners:
-
-                @pl.when(z == owner)
-                def _(side=side, owner=owner):
-                    total = part[tt]
-                    number = counts[tt]
-                    for source in range(n):
-                        if source != owner:
-                            for copy in code_copies(side, tt, source):
-                                copy.wait_recv()
-                            code = code_in[tt, source].astype(jnp.int32).astype(jnp.float32)
-                            total = total + code * scale_in[tt, source, :, :half]
-                            number = number + scale_in[tt, source, :, half:]
-                    part[tt] = total
-                    counts[tt] = number
+            row = jnp.where(tt < early, tt, tt - early)
+            for side in range(2):
+                for owner, is_early in ((ends[side][1], True), (middles[side][1], False)):
+                    right_time = tt < early if is_early else tt >= early
+
+                    @pl.when(jnp.logical_and(z == owner, right_time))
+                    def _(side=side, owner=owner):
+                        total = part[row]
+                        number = counts[row]
+                        for source in range(n):
+                            if source != owner:
+                                for copy in code_copies(side, tt, source):
+                                    copy.wait_recv()
+                                code = code_in[tt, source].astype(jnp.int32)
+                                code = code.astype(jnp.float32)
+                                total = total + code * scale_in[tt, source, :, :half]
+                                number = number + scale_in[tt, source, :, half:]
+                        part[row] = total
+                        counts[row] = number
 
         @pl.when(s < steps)
         def _():
-            one_beam(steps + s)
-            pair_copy(s).start()
+            one_beam(mine(s))
 
         return carry
 
+    @pl.when(jnp.logical_not(is_mid))
+    def _():
+        pl.semaphore_wait(hello, 1)
+
     lax.fori_loop(0, steps + LAG, slot, 0)
 
-    items = steps * side_chan
-
-    def send_copy(d, side):
+    items = pay.shape[0]
+
+    def send_copy(d, side, buf, which):
         return pltpu.make_async_remote_copy(
-            src_ref=pay,
-            dst_ref=gat.at[side, c],
+            src_ref=pay.at[: buf.shape[2]],
+            dst_ref=buf.at[side, c],
             send_sem=gsend.at[d],
-            recv_sem=grecv.at[side, c],
+            recv_sem=grecv.at[which, side, c],
             device_id={"rng": lax.rem(me + d, size)},
             device_id_type=MESH,
         )
 
-    @pl.when(is_mid)
-    def _():
-        solve_kernel(part, solved, stack, turned, hr, hi, xr, xi, yr, yi)
-        flipped = solved[...].T
-        scaled = []
-        for t in range(steps):
-            scaled.append(flipped[side_chan * t : side_chan * (t + 1)] * counts[t])
-        full = jnp.concatenate(scaled, 0)
-        lane = lax.broadcasted_iota(jnp.int32, (items, lanes), 1)
-        hi_part = full.astype(jnp.bfloat16).astype(jnp.float32)
-        rest = full - hi_part
-        mid_part = rest.astype(jnp.bfloat16).astype(jnp.float32)
-        lo_part = rest - mid_part
-        split = jnp.where(
-            lane == 2 * dof + 1, mid_part, jnp.where(lane == 2 * dof + 2, lo_part, hi_part)
-        )
-        pay[...] = split.astype(jnp.bfloat16)
-        for side, owner in owners:
+    solve_kernel(part, solved, stack, turned, hr, hi, xr, xi, yr, yi)
+    flipped = solved[...].T
+    scaled = []
+    for t in range(items // side_chan):
+        scaled.append(flipped[side_chan * t : side_chan * (t + 1)] * counts[t])
+    full = jnp.concatenate(scaled, 0)
+    lane = lax.broadcasted_iota(jnp.int32, (items, lanes), 1)
+    hi_part = full.astype(jnp.bfloat16).astype(jnp.float32)
+    rest = full - hi_part
+    mid_part = rest.astype(jnp.bfloat16).astype(jnp.float32)
+    lo_part = rest - mid_part
+    split = jnp.where(
+        lane == 2 * dof + 1, mid_part, jnp.where(lane == 2 * dof + 2, lo_part, hi_part)
+    )
+    pay[...] = split.astype(jnp.bfloat16)
+    for which, (places, buf) in enumerate(((ends, gat_e), (middles, gat_l))):
+        for side, owner in places:
 
             @pl.when(z == owner)
-            def _(side=side):
+            def _(side=side, buf=buf, which=which):
                 for d in range(1, size):
-                    send_copy(d, side).start()
-                gat[side, c] = pay[...]
+                    send_copy(d, side, buf, which).start()
+                buf[side, c] = pay[: buf.shape[2]]
 
     freq = (lax.broadcasted_iota(jnp.int32, (num_chan, taps), 1) // num_sel).astype(jnp.float32)
     centres = chan_ref[...].astype(jnp.float32)
@@ -842,7 +873,7 @@
             device_id_type=MESH,
         )
 
-    def one_power(b, t, core):
+    def one_power(b, tiles, t, core):
         start = pl.multiple_of(t * side_chan, side_chan)
         both = [tiles[side, core, pl.ds(start, side_chan), :] for side in range(2)]
         wide = jnp.concatenate(both, 0)
@@ -880,27 +911,33 @@
         def _():
             tile_copy(0, b).start()
 
-    for side, owner in owners:
-        for core in range(2):
-
-            @pl.when(me != 2 * owner + core)
-            def _(side=side, core=core):
-                pltpu.make_async_remote_copy(
-                    src_ref=pay,
-                    dst_ref=gat.at[side, core],
-                    send_sem=gsend.at[0],
-                    recv_sem=grecv.at[side, core],
-                    device_id={"rng": ahead},
-                    device_id_type=MESH,
-                ).wait_recv()
-
-            tiles[side, core] = jnp.dot(
-                gat[side, core], spread_ref[...], preferred_element_type=jnp.float32
-            )
-
-    def power(i, carry):
-        one_power(i, steps - 1 - i, 0)
-        one_power(beams - 1 - i, steps - 1 - i, 1)
+    def spread_weights(which, places, buf, tiles):
+        for side, owner in places:
+            for core in range(2):
+
+                @pl.when(me != 2 * owner + core)
+                def _(side=side, core=core):
+                    pltpu.make_async_remote_copy(
+                        src_ref=pay.at[: buf.shape[2]],
+                        dst_ref=buf.at[side, core],
+                        send_sem=gsend.at[0],
+                        recv_sem=grecv.at[which, side, core],
+                        device_id={"rng": ahead},
+                        device_id_type=MESH,
+                    ).wait_recv()
+
+                tiles[side, core] = jnp.dot(
+                    buf[side, core], spread_ref[...], preferred_element_type=jnp.float32
+                )
+
+    def early_power(t, carry):
+        one_power(steps - 1 - t, tiles_e, t, 0)
+        one_power(steps + t, tiles_e, t, 1)
+        return carry
+
+    def late_power(i, carry):
+        one_power(i, tiles_l, late - 1 - i, 0)
+        one_power(beams - 1 - i, tiles_l, late - 1 - i, 1)
 
         @pl.when(i == 0)
         def _():
@@ -917,7 +954,10 @@
 
         return carry
 
-    lax.fori_loop(0, steps, power, 0)
+    spread_weights(0, ends, gat_e, tiles_e)
+    lax.fori_loop(0, early, early_power, 0)
+    spread_weights(1, middles, gat_l, tiles_l)
+    lax.fori_loop(0, late, late_power, 0)
 
     lane = lax.broadcasted_iota(jnp.int32, (num_chan, cells), 1)
 
@@ -927,20 +967,31 @@
         fore = pltpu.roll(jnp.where(lane == 0, pl_right[i], mid), cells - 1, 1)
         return back + mid + fore
 
-    for b in range(beams):
-
-        @pl.when(me > 0)
-        def _(b=b):
-            tile_copy(1, b).wait_recv()
-
-        @pl.when(me < size - 1)
-        def _(b=b):
-            tile_copy(0, b).wait_recv()
-
-    for b in range(beams):
-        rows[b + 1] = row_sum(b + 1)
-    for b in range(1, beams - 1):
+    def finish(group):
+        for b in group:
+
+            @pl.when(me > 0)
+            def _(b=b):
+                tile_copy(1, b).wait_recv()
+
+            @pl.when(me < size - 1)
+            def _(b=b):
+                tile_copy(0, b).wait_recv()
+
+        for b in group:
+            rows[b + 1] = row_sum(b + 1)
+
+    def smooth(b):
         out_ref[b] = (rows[b] + rows[b + 1] + rows[b + 2]) / 9.0
+
+    finish(range(late, beams - late))
+    for b in range(late + 1, beams - late - 1):
+        smooth(b)
+    outer = [*range(late), *range(beams - late, beams)]
+    finish(outer)
+    for b in range(1, late + 1):
+        smooth(b)
+        smooth(beams - 1 - b)
     for up in range(2):
         az_copy(up).wait_recv()
 
@@ -952,26 +1003,30 @@
         def _(up=up):
             corner_copy(up, 0).wait_recv()
 
-    out_ref[0] = (row_sum(0) + rows[1] + rows[2]) / 9.0
-    out_ref[beams - 1] = (rows[beams - 1] + rows[beams] + row_sum(beams + 1)) / 9.0
+    rows[0] = row_sum(0)
+    rows[beams + 1] = row_sum(beams + 1)
+    smooth(0)
+    smooth(beams - 1)
 
     for i in range(steps):
         low_copy(i).wait_send()
         high_copy(i).wait_send()
         pair_copy(i).wait_send()
-        for side, owner in owners:
-
-            @pl.when(z != owner)
+        for side in range(2):
+
+            @pl.when(z != owner_of(side, i))
             def _(side=side, i=i):
                 for copy in code_copies(side, i, z):
                     copy.wait_send()
 
     mask_copy.wait_send()
 
-    @pl.when(is_mid)
-    def _():
-        for d in range(1, size):
-            send_copy(d, 0).wait_send()
+    for which, (buf, here) in enumerate(((gat_e, jnp.logical_not(is_mid)), (gat_l, is_mid))):
+
+        @pl.when(here)
+        def _(buf=buf, which=which):
+            for d in range(1, size):
+                send_copy(d, 0, buf, which).wait_send()
 
     for up in range(2):
         az_copy(up).wait_send()
@@ -986,7 +1041,7 @@
                 corner_copy(up, side).wait_send()
 
 
-def chain(echoes, arc_start, arc_offsets, doppler_bins, steer_angles, train_mask):
+def chain(echoes, arc_start, arc_offsets, doppler_bins, steer_angles, train_mask, early):
     columns, num_pulses, cells = echoes.shape[1:]
     num_sel = arc_offsets.shape[1]
     num_chan = doppler_bins.shape[1]
@@ -999,7 +1054,9 @@
     w = width // steps
     side_chan = num_chan // 2
     half = side_chan * dof
-    items = steps * side_chan
+    late = steps - early
+    most = max(early, late)
+    items = most * side_chan
     lanes = 128
     with jax.ensure_compile_time_eval():
         table_re, table_im = doppler_table(num_pulses)
@@ -1039,7 +1096,7 @@
         vm((steps, 2, 1, half + lanes), f32),
         vm((steps, n, dof, half), i16),
         vm((steps, n, 1, half + lanes), f32),
-        vm((steps, dof, half), f32),
+        vm((most, dof, half), f32),
         vm((lanes, lanes), f32),
         vm((dof, items, dof), f32),
         vm((dof, dof, items), f32),
@@ -1051,10 +1108,12 @@
         vm((dof, items), f32),
         vm((2, beams, cells), f32),
         vm((beams, lanes), f32),
-        vm((steps, 1, lanes), f32),
+        vm((most, 1, lanes), f32),
         vm((items, lanes), bf16),
-        vm((2, 2, items, lanes), bf16),
-        vm((2, 2, items, spread.shape[1]), f32),
+        vm((2, 2, early * side_chan, lanes), bf16),
+        vm((2, 2, late * side_chan, lanes), bf16),
+        vm((2, 2, early * side_chan, spread.shape[1]), f32),
+        vm((2, 2, late * side_chan, spread.shape[1]), f32),
         vm((beams + 2,) + tile, f32),
         vm((beams + 2,) + tile, f32),
         vm((beams + 2,) + tile, f32),
@@ -1069,7 +1128,8 @@
         dma,
         dma,
         dma((size,)),
-        dma((2, 2)),
+        dma((2, 2, 2)),
+        pltpu.SemaphoreType.REGULAR,
         dma((2, beams)),
         dma((2, beams)),
         dma((2,)),
@@ -1078,7 +1138,7 @@
         dma((2, 2)),
     ]
     return pl.pallas_call(
-        chain_kernel,
+        functools.partial(chain_kernel, early),
         in_specs=[pl.BlockSpec(memory_space=pl.ANY)] * 8,
         out_specs=pl.BlockSpec(memory_space=vm),
         out_shape=jax.ShapeDtypeStruct((beams,) + tile, f32),
@@ -1124,8 +1184,12 @@
         and 2 * dof + 8 <= 128
         and dof % 16 == 0
         and pairs * (chan_count // 2) <= 128
+        and pairs > LATE
+        and rng_size // 2 > 3
     ):
-        return chain(echoes, arc_start, arc_offsets, doppler_bins, steer_angles, train_mask)
+        return chain(
+            echoes, arc_start, arc_offsets, doppler_bins, steer_angles, train_mask, pairs - LATE
+        )
     table_re, table_im = doppler_table(num_pulses)
     table = jnp.concatenate(
         [jnp.concatenate([table_re, -table_im], 1), jnp.concatenate([table_im, table_re], 1)], 0

time: 57.6 us -> 55.4 us (0.962)
  Pallas kernels: 55.8 us -> 53.6 us
    pallas_call x1, Pallas kernels: 55.8 us -> 53.6 us  [chain(): pl.pallas_call(functools.partial(chain_kernel, early), in_specs=[pl.Block...]
where the time goes in v2:
time: 55.4 us; the launch traced here: 55.2 us
  Pallas kernels  53.6 us (97%)
  local copies, waits for them, and re-layouts  1.57 us (3%)
    pallas_call x1, Pallas kernels, chain(): pl.pallas_call(functools.partial(chain_kernel, early), in_specs=[pl.Block...  53.6 us
    unnamed x1, local copies, waits for them, and re-layouts  1.57 us

profile of v2, /device:TPU:1, one launch (start us, length us, event | category | flops | bytes accessed | tf_op | source)
XLA Modules:
  0.0 55.2 jit_solution(12166977581805886718)
XLA Ops:
  0.0 53.6 %chain.1 = f32[16,16,128]{2,1,0:T(8,128)} custom-call(s32[64]{0:T(128)} %start_hbm.1, s32[16,64]{1,0:T(8,128)} %bitcast.4, s32[16,64]{1,0:T(8,128)} %bitcast.5, s32[1,16]{1,0:T(1,128)} %bitcast.7, f32[16,64]{1,0:T(8,128)} %bitcast.6, bf16[2,64,32,128]{3,2,1,0:T(8,128)(2,1)} %echoes.1, bf16[64,64]{1,0:T(8,128)(2,1)} %constant.5.clone.table_hbm, ...), custom_call_target="tpu_custom_call" | custom-call | tf_op jit(solution)/shard_map/chain/pallas_call | solution.py:1140
  53.6 1.6 %copy.10 = f32[16,16,128]{2,1,0:T(8,128)} copy(f32[16,16,128]{2,1,0:T(8,128)} %chain.1) | data formatting | bytes 262144

commit v3 on v2

--- a/solution.py
+++ b/solution.py
@@ -19,7 +19,7 @@
 CHAIN_VMEM = 66_200_000
 CODE_TOP = 32000.0
 LAG = 3
-LATE = 2
+LATE = 4
 
 
 def doppler_table(num_pulses):
@@ -121,6 +121,7 @@
             pivot = 1.0 / hr[k, pl.ds(k, 1), :]
             rr = [hr[k, 8 * b : 8 * b + 8, :] for b in range(kb, nb)]
             ri = [hi[k, 8 * b : 8 * b + 8, :] for b in range(kb, nb)]
+            rs = [x + y for x, y in zip(rr, ri, strict=True)]
             gr = jnp.broadcast_to(yr[pl.ds(k, 1), :], (8, lanes))
             gi = jnp.broadcast_to(yi[pl.ds(k, 1), :], (8, lanes))
             for ib in range(kb, nb):
@@ -130,18 +131,22 @@
                     live = sub + 8 * kb > k
                     fr = jnp.where(live, fr, 0.0)
                     fi = jnp.where(live, fi, 0.0)
+                fs = fr + fi
+                fd = fi - fr
                 own = slice(8 * ib, 8 * ib + 8)
                 yr[own, :] = yr[own, :] - (fr * gr - fi * gi)
                 yi[own, :] = yi[own, :] - (fr * gi + fi * gr)
                 for s in range(8):
                     i = 8 * ib + s
                     cr = jnp.broadcast_to(fr[s : s + 1], (8, lanes))
-                    ci = jnp.broadcast_to(fi[s : s + 1], (8, lanes))
+                    cs = jnp.broadcast_to(fs[s : s + 1], (8, lanes))
+                    cd = jnp.broadcast_to(fd[s : s + 1], (8, lanes))
                     for b in range(ib, nb):
                         pr, pi = rr[b - kb], ri[b - kb]
                         sl = slice(8 * b, 8 * b + 8)
-                        hr[i, sl, :] = hr[i, sl, :] - (cr * pr - ci * pi)
-                        hi[i, sl, :] = hi[i, sl, :] - (cr * pi + ci * pr)
+                        both = cr * rs[b - kb]
+                        hr[i, sl, :] = (hr[i, sl, :] - both) + cs * pi
+                        hi[i, sl, :] = (hi[i, sl, :] - both) - cd * pr
             return carry
 
         lax.fori_loop(8 * kb, 8 * kb + 8, step, 0)
@@ -475,7 +480,7 @@
     echoes,
     table_hbm,
     spread_hbm,
-    out_ref,
+    out_hbm,
     start_ref,
     offs_ref,
     bins_ref,
@@ -486,8 +491,7 @@
     spread_ref,
     turn,
     ext,
-    low,
-    high,
+    halo,
     v_all,
     gram,
     pair,
@@ -517,7 +521,9 @@
     pl_left,
     pl_right,
     rows,
+    out_ref,
     esem,
+    osem,
     hsend,
     hrecv,
     psend,
@@ -533,7 +539,6 @@
     lrecv,
     tsend,
     trecv,
-    asend,
     arecv,
 ):
     me = lax.axis_index("rng")
@@ -543,7 +548,7 @@
     n = size // 2
     z = me // 2
     c = lax.rem(me, 2)
-    beams, num_chan, cells = out_ref.shape
+    beams, num_chan, cells = out_hbm.shape
     columns = echoes.shape[1]
     pulses = echoes.shape[2]
     num_sel = offs_ref.shape[0]
@@ -605,12 +610,15 @@
     part[...] = jnp.zeros(part.shape, jnp.float32)
     pl.semaphore_wait(barrier, 3 + jnp.where(is_mid, n - 1, 2))
 
+    def all_of(ref, sem):
+        pltpu.make_async_copy(ref, ref, sem).wait()
+
     def low_copy(i):
         return pltpu.make_async_remote_copy(
             src_ref=echoes.at[:, pl.ds(columns - w * (i + 1), w)],
-            dst_ref=low.at[i],
-            send_sem=hsend.at[0, i],
-            recv_sem=hrecv.at[0, i],
+            dst_ref=halo.at[i, 0],
+            send_sem=hsend,
+            recv_sem=hrecv.at[i],
             device_id={"az": az_next},
             device_id_type=MESH,
         )
@@ -618,9 +626,9 @@
     def high_copy(i):
         return pltpu.make_async_remote_copy(
             src_ref=echoes.at[:, pl.ds(w * i, w)],
-            dst_ref=high.at[i],
-            send_sem=hsend.at[1, i],
-            recv_sem=hrecv.at[1, i],
+            dst_ref=halo.at[i, 1],
+            send_sem=hsend,
+            recv_sem=hrecv.at[i],
             device_id={"az": az_prev},
             device_id_type=MESH,
         )
@@ -668,14 +676,16 @@
         return jnp.where(c == 0, steps + t, steps - 1 - t)
 
     def owner_of(side, t):
-        far, near = (n - 1, mid_r) if side else (0, mid_l)
-        return jnp.where(t < early, far, near)
+        return jnp.where(t < early, side * (n - 1), mid_l + side)
+
+    def row_of(t):
+        return jnp.where(t < early, t, t - early)
 
     def pair_copy(t):
         return pltpu.make_async_remote_copy(
             src_ref=gram.at[theirs(t)],
             dst_ref=pair.at[t],
-            send_sem=psend.at[t],
+            send_sem=psend,
             recv_sem=precv.at[t],
             device_id={"rng": mate},
             device_id_type=MESH,
@@ -685,10 +695,10 @@
         owner = 2 * owner_of(side, t) + c
         return [
             pltpu.make_async_remote_copy(
-                src_ref=src.at[t, side],
-                dst_ref=dst.at[t, source],
-                send_sem=dsend.at[i, t, side],
-                recv_sem=drecv.at[i, t, source],
+                src_ref=src.at[2 * t + side],
+                dst_ref=dst.at[row_of(t), source],
+                send_sem=dsend.at[i],
+                recv_sem=drecv.at[i, row_of(t)],
                 device_id={"rng": owner},
                 device_id_type=MESH,
             )
@@ -727,10 +737,9 @@
     def slot(s, carry):
         @pl.when(s < steps)
         def _():
-            low_copy(s).wait_recv()
-            high_copy(s).wait_recv()
-            ext[:, pl.ds(width - w * (s + 1), w)] = low[s]
-            ext[:, pl.ds(width + columns + w * s, w)] = high[s]
+            all_of(halo.at[s], hrecv.at[s])
+            ext[:, pl.ds(width - w * (s + 1), w)] = halo[s, 0]
+            ext[:, pl.ds(width + columns + w * s, w)] = halo[s, 1]
             one_beam(theirs(s))
             pair_copy(s).start()
 
@@ -741,7 +750,7 @@
             pair_copy(t).wait_recv()
             own = mine(t)
             number = totals[pl.ds(own, 1), :]
-            row = jnp.where(t < early, t, t - early)
+            row = row_of(t)
             for side in range(2):
                 total = gram[own, side] + pair[t, side]
                 owner = owner_of(side, t)
@@ -756,9 +765,15 @@
                     top = jnp.max(jnp.abs(total), 0, keepdims=True)
                     top = jnp.maximum(top, 1e-30)
                     code = jnp.round(total * (CODE_TOP / top))
-                    coded[t, side] = code.astype(jnp.int32).astype(jnp.int16)
-                    scale[t, side, :, :half] = top * (1.0 / CODE_TOP)
-                    scale[t, side, :, half:] = number
+                    coded[2 * t + side] = code.astype(jnp.int32).astype(jnp.int16)
+                    scale[2 * t + side, :, :half] = top * (1.0 / CODE_TOP)
+                    scale[2 * t + side, :, half:] = number
+
+            far = jnp.where(z < n // 2, 1, 0)
+            for side in (far, 1 - far):
+
+                @pl.when(z != owner_of(side, t))
+                def _(side=side):
                     for copy in code_copies(side, t, z):
                         copy.start()
 
@@ -766,7 +781,7 @@
 
         @pl.when(jnp.logical_and(tt >= 0, tt < steps))
         def _():
-            row = jnp.where(tt < early, tt, tt - early)
+            row = row_of(tt)
             for side in range(2):
                 for owner, is_early in ((ends[side][1], True), (middles[side][1], False)):
                     right_time = tt < early if is_early else tt >= early
@@ -775,14 +790,14 @@
                     def _(side=side, owner=owner):
                         total = part[row]
                         number = counts[row]
+                        all_of(code_in.at[row, pl.ds(0, n - 1)], drecv.at[0, row])
+                        all_of(scale_in.at[row, pl.ds(0, n - 1)], drecv.at[1, row])
                         for source in range(n):
                             if source != owner:
-                                for copy in code_copies(side, tt, source):
-                                    copy.wait_recv()
-                                code = code_in[tt, source].astype(jnp.int32)
+                                code = code_in[row, source].astype(jnp.int32)
                                 code = code.astype(jnp.float32)
-                                total = total + code * scale_in[tt, source, :, :half]
-                                number = number + scale_in[tt, source, :, half:]
+                                total = total + code * scale_in[row, source, :, :half]
+                                number = number + scale_in[row, source, :, half:]
                         part[row] = total
                         counts[row] = number
 
@@ -802,10 +817,10 @@
 
     def send_copy(d, side, buf, which):
         return pltpu.make_async_remote_copy(
-            src_ref=pay.at[: buf.shape[2]],
-            dst_ref=buf.at[side, c],
-            send_sem=gsend.at[d],
-            recv_sem=grecv.at[which, side, c],
+            src_ref=pay.at[: buf.shape[1]],
+            dst_ref=buf.at[2 * side + c],
+            send_sem=gsend.at[min((d - 1) // 4 + (d - 1) // 6, 2)],
+            recv_sem=grecv.at[which],
             device_id={"rng": lax.rem(me + d, size)},
             device_id_type=MESH,
         )
@@ -832,19 +847,19 @@
             def _(side=side, buf=buf, which=which):
                 for d in range(1, size):
                     send_copy(d, side, buf, which).start()
-                buf[side, c] = pay[: buf.shape[2]]
+                buf[2 * side + c] = pay[: buf.shape[1]]
 
     freq = (lax.broadcasted_iota(jnp.int32, (num_chan, taps), 1) // num_sel).astype(jnp.float32)
     centres = chan_ref[...].astype(jnp.float32)
 
-    def tile_copy(side, b):
+    def tile_copy(side, b, group):
         target = ahead if side else behind
         buf = pl_left if side else pl_right
         return pltpu.make_async_remote_copy(
             src_ref=pw.at[b + 1],
             dst_ref=buf.at[b + 1],
-            send_sem=lsend.at[side, b],
-            recv_sem=lrecv.at[side, b],
+            send_sem=lsend.at[side],
+            recv_sem=lrecv.at[side, group],
             device_id={"rng": target},
             device_id_type=MESH,
         )
@@ -853,8 +868,8 @@
         return pltpu.make_async_remote_copy(
             src_ref=pw.at[beams if up else 1],
             dst_ref=pw.at[0 if up else beams + 1],
-            send_sem=tsend.at[up],
-            recv_sem=trecv.at[up],
+            send_sem=tsend,
+            recv_sem=trecv,
             device_id={"az": az_next if up else az_prev},
             device_id_type=MESH,
         )
@@ -864,8 +879,8 @@
         return pltpu.make_async_remote_copy(
             src_ref=pw.at[beams if up else 1],
             dst_ref=buf.at[0 if up else beams + 1],
-            send_sem=asend.at[up, side],
-            recv_sem=arecv.at[up, side],
+            send_sem=lsend.at[side],
+            recv_sem=arecv.at[side],
             device_id={
                 "az": az_next if up else az_prev,
                 "rng": ahead if side else behind,
@@ -873,9 +888,9 @@
             device_id_type=MESH,
         )
 
-    def one_power(b, tiles, t, core):
+    def one_power(b, tiles, t, core, group):
         start = pl.multiple_of(t * side_chan, side_chan)
-        both = [tiles[side, core, pl.ds(start, side_chan), :] for side in range(2)]
+        both = [tiles[2 * side + core, pl.ds(start, side_chan), :] for side in range(2)]
         wide = jnp.concatenate(both, 0)
         tail = wide[:, 2 * BINS * lanes :]
         quiet = tail[:, :1] + tail[:, 1:2] + tail[:, 2:3]
@@ -905,39 +920,33 @@
 
         @pl.when(me < size - 1)
         def _():
-            tile_copy(1, b).start()
+            tile_copy(1, b, group).start()
 
         @pl.when(me > 0)
         def _():
-            tile_copy(0, b).start()
-
-    def spread_weights(which, places, buf, tiles):
-        for side, owner in places:
-            for core in range(2):
-
-                @pl.when(me != 2 * owner + core)
-                def _(side=side, core=core):
-                    pltpu.make_async_remote_copy(
-                        src_ref=pay.at[: buf.shape[2]],
-                        dst_ref=buf.at[side, core],
-                        send_sem=gsend.at[0],
-                        recv_sem=grecv.at[which, side, core],
-                        device_id={"rng": ahead},
-                        device_id_type=MESH,
-                    ).wait_recv()
-
-                tiles[side, core] = jnp.dot(
-                    buf[side, core], spread_ref[...], preferred_element_type=jnp.float32
-                )
+            tile_copy(0, b, group).start()
+
+    def spread_weights(which, buf, tiles):
+        mine_too = is_mid if which else jnp.logical_not(is_mid)
+        others = 2 * len(middles)
+        for own in range(2):
+
+            @pl.when(mine_too if own else jnp.logical_not(mine_too))
+            def _(own=own):
+                all_of(buf.at[pl.ds(0, others - own)], grecv.at[which])
+
+        flat = buf[...].reshape(others * buf.shape[1], lanes)
+        wide = jnp.dot(flat, spread_ref[...], preferred_element_type=jnp.float32)
+        tiles[...] = wide.reshape(tiles.shape)
 
     def early_power(t, carry):
-        one_power(steps - 1 - t, tiles_e, t, 0)
-        one_power(steps + t, tiles_e, t, 1)
+        one_power(steps - 1 - t, tiles_e, t, 0, 0)
+        one_power(steps + t, tiles_e, t, 1, 0)
         return carry
 
     def late_power(i, carry):
-        one_power(i, tiles_l, late - 1 - i, 0)
-        one_power(beams - 1 - i, tiles_l, late - 1 - i, 1)
+        one_power(i, tiles_l, late - 1 - i, 0, 1)
+        one_power(beams - 1 - i, tiles_l, late - 1 - i, 1, 1)
 
         @pl.when(i == 0)
         def _():
@@ -954,9 +963,9 @@
 
         return carry
 
-    spread_weights(0, ends, gat_e, tiles_e)
+    spread_weights(0, gat_e, tiles_e)
     lax.fori_loop(0, early, early_power, 0)
-    spread_weights(1, middles, gat_l, tiles_l)
+    spread_weights(1, gat_l, tiles_l)
     lax.fori_loop(0, late, late_power, 0)
 
     lane = lax.broadcasted_iota(jnp.int32, (num_chan, cells), 1)
@@ -967,16 +976,14 @@
         fore = pltpu.roll(jnp.where(lane == 0, pl_right[i], mid), cells - 1, 1)
         return back + mid + fore
 
-    def finish(group):
-        for b in group:
-
-            @pl.when(me > 0)
-            def _(b=b):
-                tile_copy(1, b).wait_recv()
-
-            @pl.when(me < size - 1)
-            def _(b=b):
-                tile_copy(0, b).wait_recv()
+    def finish(which, group):
+        @pl.when(me > 0)
+        def _():
+            all_of(pl_left.at[pl.ds(0, len(group))], lrecv.at[1, which])
+
+        @pl.when(me < size - 1)
+        def _():
+            all_of(pl_right.at[pl.ds(0, len(group))], lrecv.at[0, which])
 
         for b in group:
             rows[b + 1] = row_sum(b + 1)
@@ -984,61 +991,65 @@
     def smooth(b):
         out_ref[b] = (rows[b] + rows[b + 1] + rows[b + 2]) / 9.0
 
-    finish(range(late, beams - late))
+    def write(first, count):
+        part_of = pl.ds(first, count)
+        copy = pltpu.make_async_copy(
+            out_ref.at[part_of], out_hbm.at[part_of], osem
+        )
+        copy.start()
+
+    finish(0, range(late, beams - late))
     for b in range(late + 1, beams - late - 1):
         smooth(b)
+    write(late + 1, beams - 2 * late - 2)
     outer = [*range(late), *range(beams - late, beams)]
-    finish(outer)
+    finish(1, outer)
     for b in range(1, late + 1):
         smooth(b)
         smooth(beams - 1 - b)
-    for up in range(2):
-        az_copy(up).wait_recv()
-
-        @pl.when(me > 0)
-        def _(up=up):
-            corner_copy(up, 1).wait_recv()
-
-        @pl.when(me < size - 1)
-        def _(up=up):
-            corner_copy(up, 0).wait_recv()
+    write(1, late)
+    write(beams - 1 - late, late)
+    all_of(pw.at[pl.ds(0, 2)], trecv)
+
+    @pl.when(me > 0)
+    def _():
+        all_of(pl_left.at[pl.ds(0, 2)], arecv.at[1])
+
+    @pl.when(me < size - 1)
+    def _():
+        all_of(pl_right.at[pl.ds(0, 2)], arecv.at[0])
 
     rows[0] = row_sum(0)
     rows[beams + 1] = row_sum(beams + 1)
     smooth(0)
     smooth(beams - 1)
-
-    for i in range(steps):
-        low_copy(i).wait_send()
-        high_copy(i).wait_send()
-        pair_copy(i).wait_send()
-        for side in range(2):
-
-            @pl.when(z != owner_of(side, i))
-            def _(side=side, i=i):
-                for copy in code_copies(side, i, z):
-                    copy.wait_send()
-
+    write(0, 1)
+    write(beams - 1, 1)
+
+    all_of(echoes, hsend)
+    all_of(pair, psend)
     mask_copy.wait_send()
-
-    for which, (buf, here) in enumerate(((gat_e, jnp.logical_not(is_mid)), (gat_l, is_mid))):
+    for own, buf, here in (
+        (early, gat_e, jnp.logical_not(is_mid)),
+        (late, gat_l, is_mid),
+    ):
 
         @pl.when(here)
-        def _(buf=buf, which=which):
-            for d in range(1, size):
-                send_copy(d, 0, buf, which).wait_send()
-
-    for up in range(2):
-        az_copy(up).wait_send()
-
+        def _(own=own, buf=buf):
+            for i, ref in enumerate((coded, scale)):
+                all_of(ref.at[pl.ds(0, 2 * steps - own)], dsend.at[i])
+            all_of(buf, gsend.at[0])
+            all_of(buf.at[pl.ds(0, 2)], gsend.at[1])
+            all_of(buf.at[0], gsend.at[2])
+
+    all_of(pw.at[pl.ds(0, 2)], tsend)
     for side in range(2):
 
         @pl.when(me < size - 1 if side else me > 0)
         def _(side=side):
-            for b in range(beams):
-                tile_copy(side, b).wait_send()
-            for up in range(2):
-                corner_copy(up, side).wait_send()
+            all_of(pw, lsend.at[side])
+
+    pltpu.make_async_copy(out_ref, out_hbm, osem).wait()
 
 
 def chain(echoes, arc_start, arc_offsets, doppler_bins, steer_angles, train_mask, early):
@@ -1087,15 +1098,14 @@
         vm(spread.shape, bf16),
         vm((2,) + steer_angles.T.shape, f32),
         vm((2, columns + 2 * width, num_pulses, cells), bf16),
-        vm((steps, 2, w, num_pulses, cells), bf16),
-        vm((steps, 2, w, num_pulses, cells), bf16),
+        vm((steps, 2, 2, w, num_pulses, cells), bf16),
         vm((beams, 2, num_pulses, num_sel, cells), bf16),
         vm((beams, 2, dof, half), f32),
         vm((steps, 2, dof, half), f32),
-        vm((steps, 2, dof, half), i16),
-        vm((steps, 2, 1, half + lanes), f32),
-        vm((steps, n, dof, half), i16),
-        vm((steps, n, 1, half + lanes), f32),
+        vm((2 * steps, dof, half), i16),
+        vm((2 * steps, 1, half + lanes), f32),
+        vm((most, n, dof, half), i16),
+        vm((most, n, 1, half + lanes), f32),
         vm((most, dof, half), f32),
         vm((lanes, lanes), f32),
         vm((dof, items, dof), f32),
@@ -1110,37 +1120,38 @@
         vm((beams, lanes), f32),
         vm((most, 1, lanes), f32),
         vm((items, lanes), bf16),
-        vm((2, 2, early * side_chan, lanes), bf16),
-        vm((2, 2, late * side_chan, lanes), bf16),
-        vm((2, 2, early * side_chan, spread.shape[1]), f32),
-        vm((2, 2, late * side_chan, spread.shape[1]), f32),
+        vm((4, early * side_chan, lanes), bf16),
+        vm((4, late * side_chan, lanes), bf16),
+        vm((4, early * side_chan, spread.shape[1]), f32),
+        vm((4, late * side_chan, spread.shape[1]), f32),
         vm((beams + 2,) + tile, f32),
         vm((beams + 2,) + tile, f32),
         vm((beams + 2,) + tile, f32),
         vm((beams + 2,) + tile, f32),
+        vm((beams,) + tile, f32),
         dma((9,)),
-        dma((2, steps)),
-        dma((2, steps)),
-        dma((steps,)),
-        dma((steps,)),
-        dma((2, steps, 2)),
-        dma((2, steps, n)),
         dma,
         dma,
-        dma((size,)),
-        dma((2, 2, 2)),
+        dma((steps,)),
+        dma,
+        dma((steps,)),
+        dma((2,)),
+        dma((2, most)),
+        dma,
+        dma,
+        dma((3,)),
+        dma((2,)),
         pltpu.SemaphoreType.REGULAR,
-        dma((2, beams)),
-        dma((2, beams)),
-        dma((2,)),
         dma((2,)),
         dma((2, 2)),
-        dma((2, 2)),
+        dma,
+        dma,
+        dma((2,)),
     ]
     return pl.pallas_call(
         functools.partial(chain_kernel, early),
         in_specs=[pl.BlockSpec(memory_space=pl.ANY)] * 8,
-        out_specs=pl.BlockSpec(memory_space=vm),
+        out_specs=pl.BlockSpec(memory_space=pl.ANY),
         out_shape=jax.ShapeDtypeStruct((beams,) + tile, f32),
         scratch_shapes=scratch,
         compiler_params=pltpu.CompilerParams(

time: 55.4 us -> 52.9 us (0.955)
  Pallas kernels: 53.6 us -> 50.8 us
    pallas_call x1, Pallas kernels: 53.6 us -> 50.8 us  [chain(): pl.pallas_call(functools.partial(chain_kernel, early), in_specs=[pl.Block...]
where the time goes in v3:
time: 52.9 us; the launch traced here: 52.4 us
  Pallas kernels  50.8 us (96%)
  local copies, waits for them, and re-layouts  1.57 us (3%)
    pallas_call x1, Pallas kernels, chain(): pl.pallas_call(functools.partial(chain_kernel, early), in_specs=[pl.Block...  50.8 us
    unnamed x1, local copies, waits for them, and re-layouts  1.57 us

profile of v3, /device:TPU:1, one launch (start us, length us, event | category | flops | bytes accessed | tf_op | source)
XLA Modules:
  0.0 52.4 jit_solution(7628736628854948092)
XLA Ops:
  0.0 50.8 %chain.1 = f32[16,16,128]{2,1,0:T(8,128)} custom-call(s32[64]{0:T(128)} %start_hbm.1, s32[16,64]{1,0:T(8,128)} %bitcast.4, s32[16,64]{1,0:T(8,128)} %bitcast.5, s32[1,16]{1,0:T(1,128)} %bitcast.7, f32[16,64]{1,0:T(8,128)} %bitcast.6, bf16[2,64,32,128]{3,2,1,0:T(8,128)(2,1)} %echoes.1, bf16[64,64]{1,0:T(8,128)(2,1)} %constant.5.clone.table_hbm, ...), custom_call_target="tpu_custom_call" | custom-call | tf_op jit(solution)/shard_map/chain/pallas_call | solution.py:1151
  50.8 1.6 %copy.10 = f32[16,16,128]{2,1,0:T(8,128)} copy(f32[16,16,128]{2,1,0:T(8,128)} %chain.1) | data formatting | bytes 262144

commit v4 on v3

--- a/solution.py
+++ b/solution.py
@@ -117,7 +117,7 @@
 
     for kb in range(nb):
 
-        def step(k, carry, kb=kb):
+        def step(k, carry, kb=kb, first=0):
             pivot = 1.0 / hr[k, pl.ds(k, 1), :]
             rr = [hr[k, 8 * b : 8 * b + 8, :] for b in range(kb, nb)]
             ri = [hi[k, 8 * b : 8 * b + 8, :] for b in range(kb, nb)]
@@ -136,7 +136,7 @@
                 own = slice(8 * ib, 8 * ib + 8)
                 yr[own, :] = yr[own, :] - (fr * gr - fi * gi)
                 yi[own, :] = yi[own, :] - (fr * gi + fi * gr)
-                for s in range(8):
+                for s in range(first + 1 if ib == kb else 0, 8):
                     i = 8 * ib + s
                     cr = jnp.broadcast_to(fr[s : s + 1], (8, lanes))
                     cs = jnp.broadcast_to(fs[s : s + 1], (8, lanes))
@@ -149,7 +149,8 @@
                         hi[i, sl, :] = (hi[i, sl, :] - both) - cd * pr
             return carry
 
-        lax.fori_loop(8 * kb, 8 * kb + 8, step, 0)
+        for first in range(8):
+            step(8 * kb + first, 0, first=first)
 
     for ib in reversed(range(nb)):
 
@@ -608,6 +609,7 @@
     pl_right[...] = jnp.zeros(pl_right.shape, jnp.float32)
     solved[...] = jnp.zeros(solved.shape, jnp.float32)
     part[...] = jnp.zeros(part.shape, jnp.float32)
+    counts[...] = jnp.zeros(counts.shape, jnp.float32)
     pl.semaphore_wait(barrier, 3 + jnp.where(is_mid, n - 1, 2))
 
     def all_of(ref, sem):
@@ -735,14 +737,6 @@
         gram[b, 1] = jnp.concatenate(packed[side_chan:], 1)
 
     def slot(s, carry):
-        @pl.when(s < steps)
-        def _():
-            all_of(halo.at[s], hrecv.at[s])
-            ext[:, pl.ds(width - w * (s + 1), w)] = halo[s, 0]
-            ext[:, pl.ds(width + columns + w * s, w)] = halo[s, 1]
-            one_beam(theirs(s))
-            pair_copy(s).start()
-
         t = s - 1
 
         @pl.when(jnp.logical_and(t >= 0, t < steps))
@@ -803,6 +797,11 @@
 
         @pl.when(s < steps)
         def _():
+            all_of(halo.at[s], hrecv.at[s])
+            ext[:, pl.ds(width - w * (s + 1), w)] = halo[s, 0]
+            ext[:, pl.ds(width + columns + w * s, w)] = halo[s, 1]
+            one_beam(theirs(s))
+            pair_copy(s).start()
             one_beam(mine(s))
 
         return carry
@@ -815,21 +814,24 @@
 
     items = pay.shape[0]
 
-    def send_copy(d, side, buf, which):
+    def send_copy(at, place, core, side, buf, which):
         return pltpu.make_async_remote_copy(
             src_ref=pay.at[: buf.shape[1]],
             dst_ref=buf.at[2 * side + c],
-            send_sem=gsend.at[min((d - 1) // 4 + (d - 1) // 6, 2)],
+            send_sem=gsend.at[at // 4 + at // 6],
             recv_sem=grecv.at[which],
-            device_id={"rng": lax.rem(me + d, size)},
+            device_id={"rng": 2 * place + core},
             device_id_type=MESH,
         )
 
     solve_kernel(part, solved, stack, turned, hr, hi, xr, xi, yr, yi)
     flipped = solved[...].T
     scaled = []
-    for t in range(items // side_chan):
+    for t in range(part.shape[0]):
         scaled.append(flipped[side_chan * t : side_chan * (t + 1)] * counts[t])
+    spare = items - len(scaled) * side_chan
+    if spare:
+        scaled.append(jnp.zeros((spare, lanes), jnp.float32))
     full = jnp.concatenate(scaled, 0)
     lane = lax.broadcasted_iota(jnp.int32, (items, lanes), 1)
     hi_part = full.astype(jnp.bfloat16).astype(jnp.float32)
@@ -844,9 +846,12 @@
         for side, owner in places:
 
             @pl.when(z == owner)
-            def _(side=side, buf=buf, which=which):
-                for d in range(1, size):
-                    send_copy(d, side, buf, which).start()
+            def _(side=side, buf=buf, which=which, owner=owner):
+                order = sorted(range(n), key=lambda place: -abs(place - owner))
+                peers = [(place, core) for place in order for core in (c, 1 - c)]
+                peers.remove((owner, c))
+                for at, (place, core) in enumerate(peers):
+                    send_copy(at, place, core, side, buf, which).start()
                 buf[2 * side + c] = pay[: buf.shape[1]]
 
     freq = (lax.broadcasted_iota(jnp.int32, (num_chan, taps), 1) // num_sel).astype(jnp.float32)
@@ -888,7 +893,7 @@
             device_id_type=MESH,
         )
 
-    def one_power(b, tiles, t, core, group):
+    def one_power(b, tiles, t, core, group, edge=None):
         start = pl.multiple_of(t * side_chan, side_chan)
         both = [tiles[2 * side + core, pl.ds(start, side_chan), :] for side in range(2)]
         wide = jnp.concatenate(both, 0)
@@ -917,6 +922,20 @@
         p0 = proj[:num_chan]
         p1 = proj[num_chan:]
         pw[b + 1] = (p0 * p0 + p1 * p1) / quiet
+        if edge is not None:
+            up, first = edge
+
+            @pl.when(first)
+            def _():
+                @pl.when(me < size - 1)
+                def _():
+                    corner_copy(up, 1).start()
+
+                @pl.when(me > 0)
+                def _():
+                    corner_copy(up, 0).start()
+
+                az_copy(up).start()
 
         @pl.when(me < size - 1)
         def _():
@@ -945,21 +964,8 @@
         return carry
 
     def late_power(i, carry):
-        one_power(i, tiles_l, late - 1 - i, 0, 1)
-        one_power(beams - 1 - i, tiles_l, late - 1 - i, 1, 1)
-
-        @pl.when(i == 0)
-        def _():
-            for up in range(2):
-                az_copy(up).start()
-
-                @pl.when(me < size - 1)
-                def _(up=up):
-                    corner_copy(up, 1).start()
-
-                @pl.when(me > 0)
-                def _(up=up):
-                    corner_copy(up, 0).start()
+        one_power(i, tiles_l, late - 1 - i, 0, 1, (0, i == 0))
+        one_power(beams - 1 - i, tiles_l, late - 1 - i, 1, 1, (1, i == 0))
 
         return carry
 
@@ -1068,6 +1074,9 @@
     late = steps - early
     most = max(early, late)
     items = most * side_chan
+    early_rows = -(-early * side_chan // 16) * 16
+    late_rows = -(-late * side_chan // 16) * 16
+    most_rows = max(early_rows, late_rows)
     lanes = 128
     with jax.ensure_compile_time_eval():
         table_re, table_im = doppler_table(num_pulses)
@@ -1119,11 +1128,11 @@
         vm((2, beams, cells), f32),
         vm((beams, lanes), f32),
         vm((most, 1, lanes), f32),
-        vm((items, lanes), bf16),
-        vm((4, early * side_chan, lanes), bf16),
-        vm((4, late * side_chan, lanes), bf16),
-        vm((4, early * side_chan, spread.shape[1]), f32),
-        vm((4, late * side_chan, spread.shape[1]), f32),
+        vm((most_rows, lanes), bf16),
+        vm((4, early_rows, lanes), bf16),
+        vm((4, late_rows, lanes), bf16),
+        vm((4, early_rows, spread.shape[1]), f32),
+        vm((4, late_rows, spread.shape[1]), f32),
         vm((beams + 2,) + tile, f32),
         vm((beams + 2,) + tile, f32),
         vm((beams + 2,) + tile, f32),

time: 52.9 us -> 51.4 us (0.972)
  Pallas kernels: 50.8 us -> 49 us
    pallas_call x1, Pallas kernels: 50.8 us -> 49 us  [chain(): pl.pallas_call(functools.partial(chain_kernel, early), in_specs=[pl.Block...]
where the time goes in v4:
time: 51.4 us; the launch traced here: 50.6 us
  Pallas kernels  49 us (95%)
  local copies, waits for them, and re-layouts  1.57 us (3%)
    pallas_call x1, Pallas kernels, chain(): pl.pallas_call(functools.partial(chain_kernel, early), in_specs=[pl.Block...  49 us
    unnamed x1, local copies, waits for them, and re-layouts  1.57 us

profile of v4, /device:TPU:1, one launch (start us, length us, event | category | flops | bytes accessed | tf_op | source)
XLA Modules:
  0.0 50.6 jit_solution(477851328967538069)
XLA Ops:
  0.0 49.0 %chain.1 = f32[16,16,128]{2,1,0:T(8,128)} custom-call(s32[64]{0:T(128)} %start_hbm.1, s32[16,64]{1,0:T(8,128)} %bitcast.4, s32[16,64]{1,0:T(8,128)} %bitcast.5, s32[1,16]{1,0:T(1,128)} %bitcast.7, f32[16,64]{1,0:T(8,128)} %bitcast.6, bf16[2,64,32,128]{3,2,1,0:T(8,128)(2,1)} %echoes.1, bf16[64,64]{1,0:T(8,128)(2,1)} %constant.5.clone.table_hbm, ...), custom_call_target="tpu_custom_call" | custom-call | tf_op jit(solution)/shard_map/chain/pallas_call | solution.py:1160
  49.1 1.6 %copy.10 = f32[16,16,128]{2,1,0:T(8,128)} copy(f32[16,16,128]{2,1,0:T(8,128)} %chain.1) | data formatting | bytes 262144

commit v5 on v4

--- a/solution.py
+++ b/solution.py
@@ -626,9 +626,10 @@
         )
 
     def high_copy(i):
+        some = w - 1 if i == steps - 1 else w
         return pltpu.make_async_remote_copy(
-            src_ref=echoes.at[:, pl.ds(w * i, w)],
-            dst_ref=halo.at[i, 1],
+            src_ref=echoes.at[:, pl.ds(w * i, some)],
+            dst_ref=halo.at[i, 1, :, pl.ds(0, some)],
             send_sem=hsend,
             recv_sem=hrecv.at[i],
             device_id={"az": az_prev},
@@ -713,7 +714,7 @@
     def one_beam(b):
         bg = az * beams + b
         first = lax.rem(start_ref[bg] - az * columns + (width + COLS), COLS)
-        first = jnp.minimum(first, ext.shape[1] - ARC)
+        first = jnp.minimum(first, ext.shape[1] - ARC - 1)
         here = blane == bg
         cosine = jnp.sum(jnp.where(here, turn[0], 0.0), 1, keepdims=True)
         sine = jnp.sum(jnp.where(here, turn[1], 0.0), 1, keepdims=True)
@@ -797,7 +798,14 @@
 
         @pl.when(s < steps)
         def _():
-            all_of(halo.at[s], hrecv.at[s])
+            @pl.when(s < steps - 1)
+            def _():
+                all_of(halo.at[s], hrecv.at[s])
+
+            @pl.when(s == steps - 1)
+            def _():
+                all_of(ext.at[0, pl.ds(0, 4 * w - 2)], hrecv.at[s])
+
             ext[:, pl.ds(width - w * (s + 1), w)] = halo[s, 0]
             ext[:, pl.ds(width + columns + w * s, w)] = halo[s, 1]
             one_beam(theirs(s))
@@ -1032,7 +1040,7 @@
     write(0, 1)
     write(beams - 1, 1)
 
-    all_of(echoes, hsend)
+    all_of(ext.at[0, pl.ds(0, 4 * width - 2)], hsend)
     all_of(pair, psend)
     mask_copy.wait_send()
     for own, buf, here in (
@@ -1196,6 +1204,7 @@
         columns == ARC
         and beam_count % 2 == 0
         and pairs * (COLS // BEAMS) == ARC // 2
+        and ARC // 2 // pairs > 1
         and rng_size == 8
         and cycle_size > 2
         and cells == 128

time: 51.4 us -> 51.4 us (level)
  no operation moved by 1% of the time
where the time goes in v5:
time: 51.4 us; the launch traced here: 50.5 us
  Pallas kernels  48.9 us (95%)
  local copies, waits for them, and re-layouts  1.57 us (3%)
    pallas_call x1, Pallas kernels, chain(): pl.pallas_call(functools.partial(chain_kernel, early), in_specs=[pl.Block...  48.9 us
    unnamed x1, local copies, waits for them, and re-layouts  1.57 us

profile of v5, /device:TPU:1, one launch (start us, length us, event | category | flops | bytes accessed | tf_op | source)
XLA Modules:
  0.0 50.5 jit_solution(3151620227782543424)
XLA Ops:
  0.0 48.9 %chain.1 = f32[16,16,128]{2,1,0:T(8,128)} custom-call(s32[64]{0:T(128)} %start_hbm.1, s32[16,64]{1,0:T(8,128)} %bitcast.4, s32[16,64]{1,0:T(8,128)} %bitcast.5, s32[1,16]{1,0:T(1,128)} %bitcast.7, f32[16,64]{1,0:T(8,128)} %bitcast.6, bf16[2,64,32,128]{3,2,1,0:T(8,128)(2,1)} %echoes.1, bf16[64,64]{1,0:T(8,128)(2,1)} %constant.5.clone.table_hbm, ...), custom_call_target="tpu_custom_call" | custom-call | tf_op jit(solution)/shard_map/chain/pallas_call | solution.py:1168
  49.0 1.6 %copy.10 = f32[16,16,128]{2,1,0:T(8,128)} copy(f32[16,16,128]{2,1,0:T(8,128)} %chain.1) | data formatting | bytes 262144
